TPU v7x, 1024 devices: a whole 8x8x8 slice. The times are simulated.
1024 devices in a mesh: wide: 64 (over y_hi, x, core), narrow: 16 (over y_lo, z).
Axes of the slice: x: 8, y: 8 (y_hi: 4, y_lo: 2; y = y_hi * 2 + y_lo), z: 8, core: 2. Of those that a mesh axis runs over, the one named last changes fastest.
Arguments:
- amplitude: float32 [65536, 256], P(('wide', 'narrow')), may hold values from -6 to 6
- tilt: float32 [3, 65536], P(None, ('wide', 'narrow')), may hold values from -3.140625 to 3.140625
- owner: int32 [65536, 1], P(('wide', 'narrow')), may hold values from 0 to 63; in each aligned block of 64 rows (0 to 63, 64 to 127, ...) at most 3 rows name the same one
- row_offset: int32 [65536], P(('wide', 'narrow')), may hold values from 0 to 496
- col_offset: int32 [65536], P(('wide', 'narrow')), may hold values from 0 to 240
Outputs:
- hologram: float32 [2, 8192, 16384], P(None, 'narrow', 'wide')
Inputs may be any that keep to these rules, and one draw needn't show every extreme that they name: `owner`: among the 64 facets of one device no tile column is named more than 3 times, and on some device one column is named exactly 3 times.
All inputs are finite; a program needn't handle non-finite values.
Results may differ from a plain program's by a relative error of at most 0.0085.
Values may be sent and summed in bfloat16 or wider, within the bound.
No kernel may reach another device: no remote copies, remote signals or barrier semaphores. Data moves between devices by JAX's collectives and lax.ppermute only.
A program may use at most 32 MiB of HBM per device.

v0:
```python
import functools
import math

import jax
import jax.numpy as jnp
from jax import lax
from jax.experimental import pallas as pl
from jax.experimental.pallas import tpu as pltpu
from jax.sharding import PartitionSpec as P

TH = 512
TW = 256
FACET = 16
DEPTH = 1280
REACH = 2
OFFSETS = 2 * REACH + 1
CAP = 3
SLOTS = OFFSETS * CAP
ROWS = 16
SPREAD = 16.0
SCALE = 1.0 / math.sqrt(TH * TW)

F32 = jnp.float32
BF16 = jnp.bfloat16
NN = (((1,), (0,)), ((), ()))
NT = (((1,), (1,)), ((), ()))


def mm(a, b, dims=NN):
    return lax.dot_general(a, b, dims, preferred_element_type=F32)


def iota(shape, dim):
    return lax.broadcasted_iota(jnp.int32, shape, dim)


def cis(angle):
    return jnp.cos(angle), jnp.sin(angle)


def signed_frequency(position, length):
    return ((position + length // 2) & (length - 1)) - length // 2


def depth_phase(position, length):
    frequency = signed_frequency(position, length)
    turns = (DEPTH * frequency * frequency) & (2 * length * length - 1)
    return turns.astype(F32) * (-math.pi / (length * length))


def reach_weight(position, length, offset):
    travel = signed_frequency(position, length).astype(F32) * (DEPTH / (length * length))
    return jnp.exp(-((travel - offset) ** 2) / SPREAD)


def from_behind(value, axis, steps):
    count = lax.axis_size(axis)
    leading, last = (max(0, -steps), min(count, count - steps))
    return lax.ppermute(value, axis, [(source, source + steps) for source in range(leading, last)])


def turn_angle(a, b, length):
    return ((a * b) & (length - 1)).astype(F32) * (2.0 * math.pi / length)


def table_kernel(fblk_ref, grow_ref, hblk_ref, kr_ref, ki_ref):
    fine_r, fine_i = cis(-turn_angle(iota((16, TW), 0), iota((16, TW), 1), TW))
    wide_r, wide_i = cis(-turn_angle(iota((16, TW), 0), iota((16, TW), 1), 16))
    for a in range(16):
        real = (wide_r[a : a + 1] * fine_r - wide_i[a : a + 1] * fine_i).astype(BF16)
        imag = (wide_r[a : a + 1] * fine_i + wide_i[a : a + 1] * fine_r).astype(BF16)
        at = 16 * a
        fblk_ref[at : at + 16, :TW] = real
        fblk_ref[at : at + 16, TW:] = -imag
        fblk_ref[TW + at : TW + at + 16, :TW] = imag
        fblk_ref[TW + at : TW + at + 16, TW:] = real
    wide_r, wide_i = cis(
        turn_angle(iota((16, TW), 0), iota((16, TW), 1), 16) + depth_phase(iota((16, TW), 1), TW)
    )
    for a in range(16):
        real = (wide_r[a : a + 1] * fine_r + wide_i[a : a + 1] * fine_i).astype(BF16)
        imag = (wide_i[a : a + 1] * fine_r - wide_r[a : a + 1] * fine_i).astype(BF16)
        at = 16 * a
        hblk_ref[at : at + 16, :TW] = real
        hblk_ref[at : at + 16, TW:] = -imag
        hblk_ref[TW + at : TW + at + 16, :TW] = imag
        hblk_ref[TW + at : TW + at + 16, TW:] = real
    fine_r, fine_i = cis(-turn_angle(iota((16, TH), 0), iota((16, TH), 1), TH))
    wide_r, wide_i = cis(-turn_angle(iota((32, TH), 0), iota((32, TH), 1), 32))
    for p in range(16):
        real = fine_r[p : p + 1] * wide_r - fine_i[p : p + 1] * wide_i
        imag = fine_r[p : p + 1] * wide_i + fine_i[p : p + 1] * wide_r
        grow_ref[32 * p : 32 * p + 32, :TH] = real.astype(BF16)
        grow_ref[32 * p : 32 * p + 32, TH:] = imag.astype(BF16)
    wide_r, wide_i = cis(
        turn_angle(iota((32, TH), 0), iota((32, TH), 1), 32) + depth_phase(iota((32, TH), 1), TH)
    )
    for q in range(32):
        real = wide_r[q : q + 1] * fine_r + wide_i[q : q + 1] * fine_i
        imag = wide_i[q : q + 1] * fine_r - wide_r[q : q + 1] * fine_i
        kr_ref[16 * q : 16 * q + 16, :] = real.astype(BF16)
        ki_ref[16 * q : 16 * q + 16, :] = imag.astype(BF16)


def make_tables():
    square = jax.ShapeDtypeStruct((TH, TH), BF16)
    return pl.pallas_call(
        table_kernel,
        out_shape=(square, jax.ShapeDtypeStruct((TH, 2 * TH), BF16), square, square, square),
        out_specs=tuple([pl.BlockSpec(memory_space=pltpu.VMEM)] * 5),
        compiler_params=pltpu.CompilerParams(vmem_limit_bytes=24 << 20),
        cost_estimate=pl.CostEstimate(flops=8_000_000, bytes_accessed=3 << 20, transcendentals=200_000),
        name="tables",
    )()


def pack_kernel(amp_ref, tilt_ref, owner_ref, row_ref, col_ref, out_ref):
    count = amp_ref.shape[0]
    total = out_ref.shape[0]
    row, col = row_ref[...], col_ref[...]
    owner = owner_ref[...].astype(F32)
    sub, lane = iota((count, count), 0), iota((count, count), 1)

    def upright(vector):
        picked = jnp.where(sub == lane, vector.astype(F32), 0.0)
        return jnp.sum(picked, axis=1, keepdims=True)

    same = (upright(owner) == owner) & (sub < lane)
    rank = jnp.sum(jnp.where(same, 1.0, 0.0), axis=0, keepdims=True)
    key = CAP * owner + rank
    amp = amp_ref[...]
    turn_v = upright(col & 15).astype(jnp.int32)
    turn_u = upright(row & 15).astype(jnp.int32)
    within = iota(amp.shape, 1) & 15
    for step in (1, 2, 4, 8):
        moved = jnp.where(
            within >= step, pltpu.roll(amp, step, 1), pltpu.roll(amp, 240 + step, 1)
        )
        amp = jnp.where((turn_v & step) != 0, moved, amp)
    for step in (1, 2, 4, 8):
        amp = jnp.where((turn_u & step) != 0, pltpu.roll(amp, 16 * step, 1), amp)
    at = iota((total, count), 0)
    wanted = CAP * (at >> 4) + (at & 15) - CAP * REACH
    wanted = jnp.where((at & 15) == SLOTS, -1, wanted).astype(F32)
    chosen = jnp.where(wanted == key, 1.0, 0.0).astype(BF16)
    placed = mm(chosen, amp.astype(BF16))
    tilt = tilt_ref[...]
    high = tilt.astype(BF16).astype(F32)
    middle = (tilt - high).astype(BF16).astype(F32)
    low = tilt - high - middle
    lines = [part[k : k + 1] for part in (high, middle, low) for k in range(3)]
    lines += [(row >> 4).astype(F32), (row & 15).astype(F32), col.astype(F32)]
    entry = iota((16, count), 0)
    extras = jnp.zeros((16, count), F32)
    for k, line in enumerate(lines):
        extras = jnp.where(entry == k, line, extras)
    mine = mm(chosen, extras.astype(BF16), NT)
    repeat = jnp.where((iota((16, 256), 1) & 15) == iota((16, 256), 0), 1.0, 0.0).astype(BF16)
    mine = mm(mine.astype(BF16), repeat)
    here = iota((total, 256), 0) & 15
    mine = jnp.where((iota((total, 256), 1) >> 4) == here, mine, 0.0)
    mine = jnp.sum(mine.reshape(total // ROWS, ROWS, 256), axis=1, keepdims=True)
    placed = placed.reshape(total // ROWS, ROWS, 256)
    result = jnp.where(iota(placed.shape, 1) == SLOTS, mine, placed)
    out_ref[...] = result.reshape(total, 256).astype(BF16)


def pack(amplitude, tilt, owner, row_offset, col_offset, wide_count):
    count = amplitude.shape[0]
    return pl.pallas_call(
        pack_kernel,
        out_shape=jax.ShapeDtypeStruct((wide_count * ROWS, 256), BF16),
        in_specs=[pl.BlockSpec(memory_space=pltpu.VMEM)] * 5,
        out_specs=pl.BlockSpec(memory_space=pltpu.VMEM),
        compiler_params=pltpu.CompilerParams(vmem_limit_bytes=24 << 20),
        name="pack",
    )(
        amplitude,
        tilt,
        owner.reshape(1, count),
        row_offset.reshape(1, count),
        col_offset.reshape(1, count),
    )


def column_kernel(inc_ref, fblk_ref, grow_ref, *refs):
    outs, (facets_lo, facets_hi, plane, total) = refs[:-4], refs[-4:]
    sources = inc_ref.shape[0] // ROWS
    lanes = CAP * sources
    facets_lo[...] = inc_ref[:, :128].astype(F32)
    facets_hi[...] = inc_ref[:, 128:].astype(F32)
    total[...] = jnp.zeros_like(total)

    def slot(i):
        pick = pl.ds(i, sources, stride=ROWS)
        return jnp.concatenate([facets_lo[pick, :], facets_hi[pick, :]], axis=1)

    extras = slot(SLOTS)
    residue = iota((16, lanes), 0).astype(F32)
    mx = iota((2 * TW, 1), 0) & (TW - 1)

    def one_column(j, carry):
        slots = [CAP * j + k for k in range(CAP)]
        amp = jnp.concatenate([slot(i) for i in slots], axis=0).T
        par = jnp.concatenate(
            [pltpu.roll(extras, 256 - 16 * i, 1)[:, :128] for i in slots], axis=0
        ).T
        tilt = [par[k : k + 1] + par[3 + k : 4 + k] + par[6 + k : 7 + k] for k in range(3)]
        block, turn_u, col = par[9:10], par[10:11], par[11:12]
        turn_v = col - 16.0 * jnp.floor(col * 0.0625)
        u = residue - turn_u
        u = jnp.where(u < 0, u + 16.0, u)
        v = residue - turn_v
        v = jnp.where(v < 0, v + 16.0, v)
        row_r, row_i = cis(tilt[0] * u + tilt[2])
        col_r, col_i = cis(tilt[1] * v)
        block = block + jnp.where(residue < turn_u, 1.0, 0.0)
        ahead = iota((TW, lanes), 0).astype(F32) - col
        window = jnp.where((ahead >= 0) & (ahead < 16.0), 1.0, 0.0).astype(BF16)
        spot = iota((128, lanes), 0)
        for group in range(4):
            part = None
            for member in range(4):
                p = 4 * group + member
                cos_p, sin_p = row_r[p : p + 1], row_i[p : p + 1]
                patch = amp[16 * p : 16 * p + 16]
                real = (patch * (cos_p * col_r - sin_p * col_i)).astype(BF16)
                imag = (patch * (cos_p * col_i + sin_p * col_r)).astype(BF16)
                spread = jnp.concatenate(
                    [jnp.concatenate([real] * 16, axis=0) * window]
                    + [jnp.concatenate([imag] * 16, axis=0) * window],
                    axis=0,
                )
                want = block[p : p + 1] + float(32 * member)
                hot = jnp.where(spot.astype(F32) == want, 1.0, 0.0).astype(BF16)
                term = mm(spread, hot, NT)
                part = term if part is None else part + term
            plane[:, 128 * group : 128 * group + 128] = part.astype(BF16)
        weight = reach_weight(mx, TW, (REACH - j).astype(F32))
        total[...] += weight * mm(fblk_ref[...], plane[...])
        return carry

    lax.fori_loop(0, OFFSETS, one_column, 0)
    rows = TW // len(outs)
    for k, out_ref in enumerate(outs):
        top = mm(total[rows * k : rows * k + rows].astype(BF16), grow_ref[...])
        bottom = mm(total[TW + rows * k : TW + rows * k + rows].astype(BF16), grow_ref[...])
        out_ref[0] = ((top[:, :TH] - bottom[:, TH:]) * SCALE).astype(BF16)
        out_ref[1] = ((top[:, TH:] + bottom[:, :TH]) * SCALE).astype(BF16)


def column_sums(incoming, fblk, grow, chunks):
    piece = jax.ShapeDtypeStruct((2, TW // chunks, TH), BF16)
    return pl.pallas_call(
        column_kernel,
        out_shape=tuple([piece] * chunks),
        in_specs=[pl.BlockSpec(memory_space=pltpu.VMEM)] * 3,
        out_specs=tuple([pl.BlockSpec(memory_space=pltpu.VMEM)] * chunks),
        scratch_shapes=[
            pltpu.VMEM((incoming.shape[0], 128), F32),
            pltpu.VMEM((incoming.shape[0], 128), F32),
            pltpu.VMEM((2 * TW, TH), BF16),
            pltpu.VMEM((2 * TW, TH), F32),
        ],
        compiler_params=pltpu.CompilerParams(vmem_limit_bytes=40 << 20),
        name="column_sums",
    )(incoming, fblk, grow)


def image_kernel(chunks, *refs):
    pieces = refs[: OFFSETS * chunks]
    hblk_ref, kr_ref, ki_ref, out_ref, band = refs[OFFSETS * chunks :]
    my = iota((1, TH), 1)
    rows = TW // chunks
    for part in range(2):
        for k in range(chunks):
            acc = None
            for at in range(OFFSETS):
                piece = pieces[OFFSETS * k + at]
                term = reach_weight(my, TH, float(at - REACH)) * piece[part].astype(F32)
                acc = term if acc is None else acc + term
            start = TW * part + rows * k
            band[start : start + rows, :] = acc.astype(BF16)
    image = mm(hblk_ref[...], band[...]).astype(BF16)
    image_r, image_i = image[:TW], image[TW:]
    out_ref[0] = (mm(kr_ref[...], image_r, NT) - mm(ki_ref[...], image_i, NT)) * SCALE
    out_ref[1] = (mm(kr_ref[...], image_i, NT) + mm(ki_ref[...], image_r, NT)) * SCALE


def image_of(pieces, hblk, kr, ki, chunks):
    return pl.pallas_call(
        functools.partial(image_kernel, chunks),
        out_shape=jax.ShapeDtypeStruct((2, TH, TW), F32),
        in_specs=[pl.BlockSpec(memory_space=pltpu.VMEM)] * (OFFSETS * chunks + 3),
        out_specs=pl.BlockSpec(memory_space=pltpu.VMEM),
        scratch_shapes=[pltpu.VMEM((2 * TW, TH), BF16)],
        compiler_params=pltpu.CompilerParams(vmem_limit_bytes=40 << 20),
        name="image",
    )(*pieces, hblk, kr, ki)


def local(amplitude, tilt, owner, row_offset, col_offset):
    chunks = 2
    wide_count = lax.axis_size("wide")
    fblk, grow, hblk, kr, ki = make_tables()
    outgoing = pack(amplitude, tilt, owner, row_offset, col_offset, wide_count)
    incoming = lax.all_to_all(
        outgoing.reshape(wide_count, ROWS, 256), "wide", split_axis=0, concat_axis=0, tiled=True
    ).reshape(wide_count * ROWS, 256)
    own = column_sums(incoming, fblk, grow, chunks)
    pieces = []
    for mine in own:
        below1 = from_behind(mine, "narrow", 1)
        above1 = from_behind(mine, "narrow", -1)
        below2 = from_behind(below1, "narrow", 1)
        above2 = from_behind(above1, "narrow", -1)
        pieces += [above2, above1, mine, below1, below2]
    return image_of(pieces, hblk, kr, ki, chunks)


def solution(mesh):
    in_specs = (
        P(("wide", "narrow"), None),
        P(None, ("wide", "narrow")),
        P(("wide", "narrow"), None),
        P(("wide", "narrow")),
        P(("wide", "narrow")),
    )
    out_specs = P(None, "narrow", "wide")
    return jax.shard_map(local, mesh=mesh, in_specs=in_specs, out_specs=out_specs, check_vma=False)
```

profile of v0, /device:TPU:22, one launch (start us, length us, event | category | flops | bytes accessed | tf_op | source)
XLA Modules:
  0.0 97.8 jit_solution(13169425975743361180)
XLA Ops:
  0.0 0.0 copy-start.3
  0.0 0.0 copy-start.4
  0.0 0.0 copy-start.5
  0.0 0.0 copy-start.6
  0.0 0.7 copy-done.3
  0.7 0.0 copy-done.4
  0.7 0.0 copy-done.5
  0.7 0.0 copy-done.6
  0.7 0.0 copy-start.2
  0.7 0.8 copy-done.2
  1.5 2.2 %pack.1 = bf16[1024,256]{1,0:T(8,128)(2,1)} custom-call(f32[64,256]{1,0:T(8,128)S(1)} %copy-done.2, f32[3,64]{1,0:T(4,128)S(1)} %copy-done.3, s32[1,64]{1,0:T(1,128)S(1)} %bitcast.6, s32[1,64]{1,0:T(1,128)S(1)} %bitcast.7, s32[1,64]{1,0:T(1,128)S(1)} %bitcast.8), custom_call_target="tpu_custom_call" | custom-call | tf_op jit(solution)/shard_map/pack/pallas_call | solution.py:170
  3.7 12.6 %all-to-all-start = ((bf16[64,16,256]{2,1,0:T(8,128)(2,1)}), bf16[64,16,256]{2,1,0:T(8,128)(2,1)S(1)}, u32[]{:S(2)}, u32[]{:S(2)}) async-start(bf16[64,16,256]{2,1,0:T(8,128)(2,1)} %bitcast.3), calls=%async_computation | async-start | bytes 1048576 | tf_op jit(solution)/shard_map/all_to_all | solution.py:307
  16.3 1.5 %tables.1 = (bf16[512,512]{1,0:T(8,128)(2,1)S(1)}, bf16[512,1024]{1,0:T(8,128)(2,1)S(1)}, bf16[512,512]{1,0:T(8,128)(2,1)S(1)}, bf16[512,512]{1,0:T(8,128)(2,1)S(1)}, bf16[512,512]{1,0:T(8,128)(2,1)S(1)}) custom-call(), custom_call_target="tpu_custom_call" | custom-call | flops 8000000 | bytes 3145728 | tf_op jit(solution)/shard_map/tables/pallas_call | solution.py:107
  17.8 0.0 copy-start
  17.8 0.8 copy-done
  18.6 16.0 %all-to-all-done = bf16[64,16,256]{2,1,0:T(8,128)(2,1)S(1)} async-done(((bf16[64,16,256]{2,1,0:T(8,128)(2,1)}), bf16[64,16,256]{2,1,0:T(8,128)(2,1)S(1)}, u32[]{:S(2)}, u32[]{:S(2)}) %all-to-all-start) | async-done | bytes 524320 | tf_op jit(solution)/shard_map/all_to_all | solution.py:307
  34.7 0.0 copy-start.1
  34.7 1.0 %copy-done.1 = bf16[512,512]{1,0:T(8,128)(2,1)S(1)} copy-done((bf16[512,512]{1,0:T(8,128)(2,1)S(1)}, bf16[512,512]{1,0:T(8,128)(2,1)}, u32[]{:S(2)}) %copy-start.1) | copy-done | bytes 524312
  35.7 10.7 %column_sums.1 = (bf16[2,128,512]{2,1,0:T(8,128)(2,1)S(1)}, bf16[2,128,512]{2,1,0:T(8,128)(2,1)S(1)}) custom-call(bf16[1024,256]{1,0:T(8,128)(2,1)S(1)} %bitcast.5, bf16[512,512]{1,0:T(8,128)(2,1)S(1)} %copy-done.1, bf16[512,1024]{1,0:T(8,128)(2,1)S(1)} %get-tuple-element.13.grow_ref), custom_call_target="tpu_custom_call" | custom-call | tf_op jit(solution)/shard_map/column_sums/pallas_call | solution.py:254
  46.5 5.2 %collective-permute-start.2 = (bf16[2,128,512]{2,1,0:T(8,128)(2,1)S(1)}, bf16[2,128,512]{2,1,0:T(8,128)(2,1)S(1)}, u32[]{:S(2)}, u32[]{:S(2)}) collective-permute-start(bf16[2,128,512]{2,1,0:T(8,128)(2,1)S(1)} %get-tuple-element.14.refs_2_), channel_id=1, source_target_pairs={{0,1},{1,2},{2,3},{3,4},{4,5},{5,6},{6,7},{7,8},{8,9},{9,10},{10,1... | collective-permute-start | bytes 786440 | tf_op jit(solution)/shard_map/ppermute | solution.py:59
  51.6 14.7 %collective-permute-start = (bf16[2,128,512]{2,1,0:T(8,128)(2,1)S(1)}, bf16[2,128,512]{2,1,0:T(8,128)(2,1)S(1)}, u32[]{:S(2)}, u32[]{:S(2)}) collective-permute-start(bf16[2,128,512]{2,1,0:T(8,128)(2,1)S(1)} %get-tuple-element.14.refs_2_), channel_id=1, source_target_pairs={{1,0},{2,1},{3,2},{4,3},{5,4},{6,5},{7,6},{8,7},{9,8},{10,9},{11,1... | collective-permute-start | bytes 786440 | tf_op jit(solution)/shard_map/ppermute | solution.py:59
  66.4 1.9 %collective-permute-start.6 = (bf16[2,128,512]{2,1,0:T(8,128)(2,1)S(1)}, bf16[2,128,512]{2,1,0:T(8,128)(2,1)S(1)}, u32[]{:S(2)}, u32[]{:S(2)}) collective-permute-start(bf16[2,128,512]{2,1,0:T(8,128)(2,1)S(1)} %get-tuple-element.15.refs_7_), channel_id=1, source_target_pairs={{0,1},{1,2},{2,3},{3,4},{4,5},{5,6},{6,7},{7,8},{8,9},{9,10},{10,1... | collective-permute-start | bytes 786440 | tf_op jit(solution)/shard_map/ppermute | solution.py:59
  68.3 6.0 %collective-permute-start.4 = (bf16[2,128,512]{2,1,0:T(8,128)(2,1)S(1)}, bf16[2,128,512]{2,1,0:T(8,128)(2,1)S(1)}, u32[]{:S(2)}, u32[]{:S(2)}) collective-permute-start(bf16[2,128,512]{2,1,0:T(8,128)(2,1)S(1)} %get-tuple-element.15.refs_7_), channel_id=1, source_target_pairs={{1,0},{2,1},{3,2},{4,3},{5,4},{6,5},{7,6},{8,7},{9,8},{10,9},{11,1... | collective-permute-start | bytes 786440 | tf_op jit(solution)/shard_map/ppermute | solution.py:59
  74.3 0.0 collective-permute-done.2.refs_3_
  74.3 1.9 %collective-permute-start.3 = (bf16[2,128,512]{2,1,0:T(8,128)(2,1)S(1)}, bf16[2,128,512]{2,1,0:T(8,128)(2,1)S(1)}, u32[]{:S(2)}, u32[]{:S(2)}) collective-permute-start(bf16[2,128,512]{2,1,0:T(8,128)(2,1)S(1)} %collective-permute-done.2.refs_3_), channel_id=1, source_target_pairs={{0,1},{1,2},{2,3},{3,4},{4,5},{5,6},{6,7},{7,8},{8,9},{9,10},{10,1... | collective-permute-start | bytes 786440 | tf_op jit(solution)/shard_map/ppermute | solution.py:59
  76.3 0.0 collective-permute-done.refs_1_
  76.3 6.0 %collective-permute-start.1 = (bf16[2,128,512]{2,1,0:T(8,128)(2,1)S(1)}, bf16[2,128,512]{2,1,0:T(8,128)(2,1)S(1)}, u32[]{:S(2)}, u32[]{:S(2)}) collective-permute-start(bf16[2,128,512]{2,1,0:T(8,128)(2,1)S(1)} %collective-permute-done.refs_1_), channel_id=1, source_target_pairs={{1,0},{2,1},{3,2},{4,3},{5,4},{6,5},{7,6},{8,7},{9,8},{10,9},{11,1... | collective-permute-start | bytes 786440 | tf_op jit(solution)/shard_map/ppermute | solution.py:59
  82.3 0.0 collective-permute-done.6.refs_8_
  82.3 1.9 %collective-permute-start.7 = (bf16[2,128,512]{2,1,0:T(8,128)(2,1)S(1)}, bf16[2,128,512]{2,1,0:T(8,128)(2,1)S(1)}, u32[]{:S(2)}, u32[]{:S(2)}) collective-permute-start(bf16[2,128,512]{2,1,0:T(8,128)(2,1)S(1)} %collective-permute-done.6.refs_8_), channel_id=1, source_target_pairs={{0,1},{1,2},{2,3},{3,4},{4,5},{5,6},{6,7},{7,8},{8,9},{9,10},{10,1... | collective-permute-start | bytes 786440 | tf_op jit(solution)/shard_map/ppermute | solution.py:59
  84.2 0.0 collective-permute-done.4.refs_6_
  84.3 6.0 %collective-permute-start.5 = (bf16[2,128,512]{2,1,0:T(8,128)(2,1)S(1)}, bf16[2,128,512]{2,1,0:T(8,128)(2,1)S(1)}, u32[]{:S(2)}, u32[]{:S(2)}) collective-permute-start(bf16[2,128,512]{2,1,0:T(8,128)(2,1)S(1)} %collective-permute-done.4.refs_6_), channel_id=1, source_target_pairs={{1,0},{2,1},{3,2},{4,3},{5,4},{6,5},{7,6},{8,7},{9,8},{10,9},{11,1... | collective-permute-start | bytes 786440 | tf_op jit(solution)/shard_map/ppermute | solution.py:59
  90.3 0.0 collective-permute-done.3.refs_4_
  90.3 0.0 collective-permute-done.1.refs_0_
  90.3 3.8 %collective-permute-done.7.refs_9_ = bf16[2,128,512]{2,1,0:T(8,128)(2,1)S(1)} collective-permute-done((bf16[2,128,512]{2,1,0:T(8,128)(2,1)S(1)}, bf16[2,128,512]{2,1,0:T(8,128)(2,1)S(1)}, u32[]{:S(2)}, u32[]{:S(2)}) %collective-permute-start.7) | collective-permute-done | bytes 262176 | tf_op jit(solution)/shard_map/ppermute | solution.py:59
  94.1 1.2 %collective-permute-done.5.refs_5_ = bf16[2,128,512]{2,1,0:T(8,128)(2,1)S(1)} collective-permute-done((bf16[2,128,512]{2,1,0:T(8,128)(2,1)S(1)}, bf16[2,128,512]{2,1,0:T(8,128)(2,1)S(1)}, u32[]{:S(2)}, u32[]{:S(2)}) %collective-permute-start.5) | collective-permute-done | bytes 262176 | tf_op jit(solution)/shard_map/ppermute | solution.py:59
  95.3 2.5 %image.1 = f32[2,512,256]{2,1,0:T(8,128)} custom-call(bf16[2,128,512]{2,1,0:T(8,128)(2,1)S(1)} %collective-permute-done.1.refs_0_, bf16[2,128,512]{2,1,0:T(8,128)(2,1)S(1)} %collective-permute-done.refs_1_, bf16[2,128,512]{2,1,0:T(8,128)(2,1)S(1)} %get-tuple-element.14.refs_2_, bf16[2,128,512]{2,1,0:T(8,128)(2,1)S(1)} %collective-permute-done.2.refs_3_, ...), custom_call_target="tpu_custom_call" | custom-call | tf_op jit(solution)/shard_map/image/pallas_call | solution.py:291
Async XLA Ops:
  0.0 0.7 copy-start.3
  0.0 0.7 copy-start.4
  0.0 0.7 copy-start.5
  0.0 0.7 copy-start.6
  0.7 0.8 copy-start.2
  3.7 30.9 %all-to-all-start = ((bf16[64,16,256]{2,1,0:T(8,128)(2,1)}), bf16[64,16,256]{2,1,0:T(8,128)(2,1)S(1)}, u32[]{:S(2)}, u32[]{:S(2)}) async-start(bf16[64,16,256]{2,1,0:T(8,128)(2,1)} %bitcast.3), calls=%async_computation | async-start | bytes 1048576 | tf_op jit(solution)/shard_map/all_to_all | solution.py:307
  17.8 0.8 copy-start
  34.7 1.0 %copy-start.1 = (bf16[512,512]{1,0:T(8,128)(2,1)S(1)}, bf16[512,512]{1,0:T(8,128)(2,1)}, u32[]{:S(2)}) copy-start(bf16[512,512]{1,0:T(8,128)(2,1)} %copy-done) | copy-start | bytes 1572868
  46.5 27.9 %collective-permute-start.2 = (bf16[2,128,512]{2,1,0:T(8,128)(2,1)S(1)}, bf16[2,128,512]{2,1,0:T(8,128)(2,1)S(1)}, u32[]{:S(2)}, u32[]{:S(2)}) collective-permute-start(bf16[2,128,512]{2,1,0:T(8,128)(2,1)S(1)} %get-tuple-element.14.refs_2_), channel_id=1, source_target_pairs={{0,1},{1,2},{2,3},{3,4},{4,5},{5,6},{6,7},{7,8},{8,9},{9,10},{10,1... | collective-permute-start | bytes 786440 | tf_op jit(solution)/shard_map/ppermute | solution.py:59
  51.6 24.6 %collective-permute-start = (bf16[2,128,512]{2,1,0:T(8,128)(2,1)S(1)}, bf16[2,128,512]{2,1,0:T(8,128)(2,1)S(1)}, u32[]{:S(2)}, u32[]{:S(2)}) collective-permute-start(bf16[2,128,512]{2,1,0:T(8,128)(2,1)S(1)} %get-tuple-element.14.refs_2_), channel_id=1, source_target_pairs={{1,0},{2,1},{3,2},{4,3},{5,4},{6,5},{7,6},{8,7},{9,8},{10,9},{11,1... | collective-permute-start | bytes 786440 | tf_op jit(solution)/shard_map/ppermute | solution.py:59
  66.4 16.0 %collective-permute-start.6 = (bf16[2,128,512]{2,1,0:T(8,128)(2,1)S(1)}, bf16[2,128,512]{2,1,0:T(8,128)(2,1)S(1)}, u32[]{:S(2)}, u32[]{:S(2)}) collective-permute-start(bf16[2,128,512]{2,1,0:T(8,128)(2,1)S(1)} %get-tuple-element.15.refs_7_), channel_id=1, source_target_pairs={{0,1},{1,2},{2,3},{3,4},{4,5},{5,6},{6,7},{7,8},{8,9},{9,10},{10,1... | collective-permute-start | bytes 786440 | tf_op jit(solution)/shard_map/ppermute | solution.py:59
  68.3 16.0 %collective-permute-start.4 = (bf16[2,128,512]{2,1,0:T(8,128)(2,1)S(1)}, bf16[2,128,512]{2,1,0:T(8,128)(2,1)S(1)}, u32[]{:S(2)}, u32[]{:S(2)}) collective-permute-start(bf16[2,128,512]{2,1,0:T(8,128)(2,1)S(1)} %get-tuple-element.15.refs_7_), channel_id=1, source_target_pairs={{1,0},{2,1},{3,2},{4,3},{5,4},{6,5},{7,6},{8,7},{9,8},{10,9},{11,1... | collective-permute-start | bytes 786440 | tf_op jit(solution)/shard_map/ppermute | solution.py:59
  74.3 16.0 %collective-permute-start.3 = (bf16[2,128,512]{2,1,0:T(8,128)(2,1)S(1)}, bf16[2,128,512]{2,1,0:T(8,128)(2,1)S(1)}, u32[]{:S(2)}, u32[]{:S(2)}) collective-permute-start(bf16[2,128,512]{2,1,0:T(8,128)(2,1)S(1)} %collective-permute-done.2.refs_3_), channel_id=1, source_target_pairs={{0,1},{1,2},{2,3},{3,4},{4,5},{5,6},{6,7},{7,8},{8,9},{9,10},{10,1... | collective-permute-start | bytes 786440 | tf_op jit(solution)/shard_map/ppermute | solution.py:59
  76.3 14.0 %collective-permute-start.1 = (bf16[2,128,512]{2,1,0:T(8,128)(2,1)S(1)}, bf16[2,128,512]{2,1,0:T(8,128)(2,1)S(1)}, u32[]{:S(2)}, u32[]{:S(2)}) collective-permute-start(bf16[2,128,512]{2,1,0:T(8,128)(2,1)S(1)} %collective-permute-done.refs_1_), channel_id=1, source_target_pairs={{1,0},{2,1},{3,2},{4,3},{5,4},{6,5},{7,6},{8,7},{9,8},{10,9},{11,1... | collective-permute-start | bytes 786440 | tf_op jit(solution)/shard_map/ppermute | solution.py:59
  82.3 11.8 %collective-permute-start.7 = (bf16[2,128,512]{2,1,0:T(8,128)(2,1)S(1)}, bf16[2,128,512]{2,1,0:T(8,128)(2,1)S(1)}, u32[]{:S(2)}, u32[]{:S(2)}) collective-permute-start(bf16[2,128,512]{2,1,0:T(8,128)(2,1)S(1)} %collective-permute-done.6.refs_8_), channel_id=1, source_target_pairs={{0,1},{1,2},{2,3},{3,4},{4,5},{5,6},{6,7},{7,8},{8,9},{9,10},{10,1... | collective-permute-start | bytes 786440 | tf_op jit(solution)/shard_map/ppermute | solution.py:59
  84.3 11.1 %collective-permute-start.5 = (bf16[2,128,512]{2,1,0:T(8,128)(2,1)S(1)}, bf16[2,128,512]{2,1,0:T(8,128)(2,1)S(1)}, u32[]{:S(2)}, u32[]{:S(2)}) collective-permute-start(bf16[2,128,512]{2,1,0:T(8,128)(2,1)S(1)} %collective-permute-done.4.refs_6_), channel_id=1, source_target_pairs={{1,0},{2,1},{3,2},{4,3},{5,4},{6,5},{7,6},{8,7},{9,8},{10,9},{11,1... | collective-permute-start | bytes 786440 | tf_op jit(solution)/shard_map/ppermute | solution.py:59
where the time goes:
time: 98.3 us; the launch traced here: 97.8 us
  starting transfers between devices  56.4 us (57%)
  waiting for transfers between devices  21 us (21%)
  Pallas kernels  16.9 us (17%)
  local copies, waits for them, and re-layouts  3.37 us (3%)
    ppermute x8, starting transfers between devices, from_behind(): lax.ppermute(value, axis, [(source, source + steps) for source in range(l...  43.7 us
    all_to_all x1, waiting for transfers between devices, local(): lax.all_to_all(outgoing.reshape(wide_count, ROWS, 256), 'wide', split_axi...  16 us
    all_to_all x1, starting transfers between devices, local(): lax.all_to_all(outgoing.reshape(wide_count, ROWS, 256), 'wide', split_axi...  12.6 us
    pallas_call x1, Pallas kernels, column_sums(): pl.pallas_call(column_kernel, out_shape=tuple([piece] * chunks), in_specs...  10.7 us
    ppermute x8, waiting for transfers between devices, from_behind(): lax.ppermute(value, axis, [(source, source + steps) for source in range(l...  5.01 us
    unnamed x14, local copies, waits for them, and re-layouts  3.37 us
    pallas_call x1, Pallas kernels, image_of(): pl.pallas_call(functools.partial(image_kernel, chunks), out_shape=jax.Sha...  2.53 us
    pallas_call x1, Pallas kernels, pack(): pl.pallas_call(pack_kernel, out_shape=jax.ShapeDtypeStruct((wide_count *...  2.18 us
  transfers between devices with their start and end apart: 9, of which 3 were waited for; matrix products, arithmetic and copies ran while one was open for 0% of the time, Pallas kernels for 2%

commit v1 on v0

v1 whole, which is shorter than its diff:
```python
import functools
import math

import jax
import jax.numpy as jnp
from jax import lax
from jax.experimental import pallas as pl
from jax.experimental.pallas import tpu as pltpu
from jax.sharding import PartitionSpec as P

TH = 512
TW = 256
FACET = 16
DEPTH = 1280
REACH = 2
OFFSETS = 2 * REACH + 1
CAP = 3
SLOTS = OFFSETS * CAP
HALF = TH // 2
ROWS = 16
SPREAD = 16.0
SCALE = 1.0 / math.sqrt(TH * TW)

F32 = jnp.float32
BF16 = jnp.bfloat16
NN = (((1,), (0,)), ((), ()))
NT = (((1,), (1,)), ((), ()))


def mm(a, b, dims=NN):
    return lax.dot_general(a, b, dims, preferred_element_type=F32)


def iota(shape, dim):
    return lax.broadcasted_iota(jnp.int32, shape, dim)


def cis(angle):
    return jnp.cos(angle), jnp.sin(angle)


def signed_frequency(position, length):
    return ((position + length // 2) & (length - 1)) - length // 2


def depth_phase(position, length):
    frequency = signed_frequency(position, length)
    turns = (DEPTH * frequency * frequency) & (2 * length * length - 1)
    return turns.astype(F32) * (-math.pi / (length * length))


def reach_weight(position, length, offset):
    travel = signed_frequency(position, length).astype(F32) * (DEPTH / (length * length))
    return jnp.exp(-((travel - offset) ** 2) / SPREAD)


def turn_angle(a, b, length):
    return ((a * b) & (length - 1)).astype(F32) * (2.0 * math.pi / length)


def table_kernel(fblk_ref, grow_a_ref, grow_b_ref, hblk_ref, kr_a_ref, ki_a_ref, kr_b_ref, ki_b_ref):
    fine_r, fine_i = cis(-turn_angle(iota((16, TW), 0), iota((16, TW), 1), TW))
    wide_r, wide_i = cis(-turn_angle(iota((16, TW), 0), iota((16, TW), 1), 16))
    for a in range(16):
        real = (wide_r[a : a + 1] * fine_r - wide_i[a : a + 1] * fine_i).astype(BF16)
        imag = (wide_r[a : a + 1] * fine_i + wide_i[a : a + 1] * fine_r).astype(BF16)
        at = 16 * a
        fblk_ref[at : at + 16, :TW] = real
        fblk_ref[at : at + 16, TW:] = -imag
        fblk_ref[TW + at : TW + at + 16, :TW] = imag
        fblk_ref[TW + at : TW + at + 16, TW:] = real
    wide_r, wide_i = cis(
        turn_angle(iota((16, TW), 0), iota((16, TW), 1), 16) + depth_phase(iota((16, TW), 1), TW)
    )
    for a in range(16):
        real = (wide_r[a : a + 1] * fine_r + wide_i[a : a + 1] * fine_i).astype(BF16)
        imag = (wide_i[a : a + 1] * fine_r - wide_r[a : a + 1] * fine_i).astype(BF16)
        at = 16 * a
        hblk_ref[at : at + 16, :TW] = real
        hblk_ref[at : at + 16, TW:] = -imag
        hblk_ref[TW + at : TW + at + 16, :TW] = imag
        hblk_ref[TW + at : TW + at + 16, TW:] = real
    fine_r, fine_i = cis(-turn_angle(iota((16, TH), 0), iota((16, TH), 1), TH))
    wide_r, wide_i = cis(-turn_angle(iota((32, TH), 0), iota((32, TH), 1), 32))
    for p in range(16):
        real = (fine_r[p : p + 1] * wide_r - fine_i[p : p + 1] * wide_i).astype(BF16)
        imag = (fine_r[p : p + 1] * wide_i + fine_i[p : p + 1] * wide_r).astype(BF16)
        at = 32 * p
        for k, ref in enumerate((grow_a_ref, grow_b_ref)):
            ref[at : at + 32, :HALF] = real[:, HALF * k : HALF * k + HALF]
            ref[at : at + 32, HALF:] = imag[:, HALF * k : HALF * k + HALF]
    wide_r, wide_i = cis(
        turn_angle(iota((32, TH), 0), iota((32, TH), 1), 32) + depth_phase(iota((32, TH), 1), TH)
    )
    for q in range(32):
        real = (wide_r[q : q + 1] * fine_r + wide_i[q : q + 1] * fine_i).astype(BF16)
        imag = (wide_i[q : q + 1] * fine_r - wide_r[q : q + 1] * fine_i).astype(BF16)
        at = 16 * q
        for k, (r_ref, i_ref) in enumerate(((kr_a_ref, ki_a_ref), (kr_b_ref, ki_b_ref))):
            r_ref[at : at + 16, :] = real[:, HALF * k : HALF * k + HALF]
            i_ref[at : at + 16, :] = imag[:, HALF * k : HALF * k + HALF]


def make_tables():
    square = jax.ShapeDtypeStruct((TH, TH), BF16)
    half = jax.ShapeDtypeStruct((TH, HALF), BF16)
    return pl.pallas_call(
        table_kernel,
        out_shape=(square, square, square, square, half, half, half, half),
        out_specs=tuple([pl.BlockSpec(memory_space=pltpu.VMEM)] * 8),
        compiler_params=pltpu.CompilerParams(vmem_limit_bytes=12 << 20),
        cost_estimate=pl.CostEstimate(flops=8_000_000, bytes_accessed=3 << 20, transcendentals=200_000),
        name="tables",
    )()


def pack_kernel(amp_ref, tilt_ref, owner_ref, row_ref, col_ref, out_ref):
    count = amp_ref.shape[0]
    total = out_ref.shape[0]
    row, col = row_ref[...], col_ref[...]
    owner = owner_ref[...].astype(F32)
    sub, lane = iota((count, count), 0), iota((count, count), 1)

    def upright(vector):
        picked = jnp.where(sub == lane, vector.astype(F32), 0.0)
        return jnp.sum(picked, axis=1, keepdims=True)

    same = (upright(owner) == owner) & (sub < lane)
    rank = jnp.sum(jnp.where(same, 1.0, 0.0), axis=0, keepdims=True)
    key = CAP * owner + rank
    amp = amp_ref[...]
    turn_v = upright(col & 15).astype(jnp.int32)
    turn_u = upright(row & 15).astype(jnp.int32)
    within = iota(amp.shape, 1) & 15
    for step in (1, 2, 4, 8):
        moved = jnp.where(
            within >= step, pltpu.roll(amp, step, 1), pltpu.roll(amp, 240 + step, 1)
        )
        amp = jnp.where((turn_v & step) != 0, moved, amp)
    for step in (1, 2, 4, 8):
        amp = jnp.where((turn_u & step) != 0, pltpu.roll(amp, 16 * step, 1), amp)
    at = iota((total, count), 0)
    wanted = CAP * (at >> 4) + (at & 15) - CAP * REACH
    wanted = jnp.where((at & 15) == SLOTS, -1, wanted).astype(F32)
    chosen = jnp.where(wanted == key, 1.0, 0.0).astype(BF16)
    old = iota((256, 256), 0)
    new = ((old >> 4) & 3) * 64 + (old >> 6) * 16 + (old & 15)
    order = jnp.where(iota((256, 256), 1) == new, 1.0, 0.0).astype(BF16)
    placed = mm(chosen, mm(amp.astype(BF16), order).astype(BF16))
    tilt = tilt_ref[...]
    high = tilt.astype(BF16).astype(F32)
    middle = (tilt - high).astype(BF16).astype(F32)
    low = tilt - high - middle
    lines = [part[k : k + 1] for part in (high, middle, low) for k in range(3)]
    lines += [(row >> 4).astype(F32), (row & 15).astype(F32), col.astype(F32)]
    entry = iota((16, count), 0)
    extras = jnp.zeros((16, count), F32)
    for k, line in enumerate(lines):
        extras = jnp.where(entry == k, line, extras)
    mine = mm(chosen, extras.astype(BF16), NT)
    repeat = jnp.where((iota((16, 256), 1) & 15) == iota((16, 256), 0), 1.0, 0.0).astype(BF16)
    mine = mm(mine.astype(BF16), repeat)
    here = iota((total, 256), 0) & 15
    mine = jnp.where((iota((total, 256), 1) >> 4) == here, mine, 0.0)
    mine = jnp.sum(mine.reshape(total // ROWS, ROWS, 256), axis=1, keepdims=True)
    placed = placed.reshape(total // ROWS, ROWS, 256)
    result = jnp.where(iota(placed.shape, 1) == SLOTS, mine, placed)
    out_ref[...] = result.reshape(total, 256).astype(BF16)


def pack(amplitude, tilt, owner, row_offset, col_offset, wide_count):
    count = amplitude.shape[0]
    return pl.pallas_call(
        pack_kernel,
        out_shape=jax.ShapeDtypeStruct((wide_count * ROWS, 256), BF16),
        in_specs=[pl.BlockSpec(memory_space=pltpu.VMEM)] * 5,
        out_specs=pl.BlockSpec(memory_space=pltpu.VMEM),
        compiler_params=pltpu.CompilerParams(vmem_limit_bytes=63 << 20),
        name="pack",
    )(
        amplitude,
        tilt,
        owner.reshape(1, count),
        row_offset.reshape(1, count),
        col_offset.reshape(1, count),
    )


def power_of(base_r, base_i, exponent, start_r, start_i):
    real, imag = start_r, start_i
    for bit in (1, 2, 4, 8):
        step = (exponent & bit) != 0
        turned_r = real * base_r - imag * base_i
        turned_i = real * base_i + imag * base_r
        real = jnp.where(step, turned_r, real)
        imag = jnp.where(step, turned_i, imag)
        base_r, base_i = base_r * base_r - base_i * base_i, 2.0 * base_r * base_i
    return real, imag


def row_transform(value, grow_ref, out_ref):
    product = mm(value, grow_ref[...])
    out_ref[0] = ((product[:TW, :HALF] - product[TW:, HALF:]) * SCALE).astype(BF16)
    out_ref[1] = ((product[:TW, HALF:] + product[TW:, :HALF]) * SCALE).astype(BF16)


def column_kernel(inc_ref, fblk_ref, grow_ref, out_ref, value_ref, facets_lo, facets_hi, param, plane, total):
    sources = inc_ref.shape[0] // ROWS
    lanes = 4 * sources
    facets_lo[...] = inc_ref[:, :128].astype(F32)
    facets_hi[...] = inc_ref[:, 128:].astype(F32)
    total[...] = jnp.zeros_like(total)
    pick = pl.ds(SLOTS, sources, stride=ROWS)
    extras = jnp.concatenate([facets_lo[pick, :], facets_hi[pick, :]], axis=1)
    entry = iota(extras.shape, 1) & 15
    tilt = extras + pltpu.roll(extras, 253, 1) + pltpu.roll(extras, 250, 1)
    tilt = jnp.where(entry < 3, tilt, pltpu.roll(tilt, 3, 1))
    turn_r, turn_i = cis(tilt)
    param[...] = jnp.where(entry < 3, turn_r, jnp.where(entry < 6, turn_i, extras))
    mx = iota((2 * TW, 1), 0) & (TW - 1)
    member = iota((8, lanes), 1) // sources
    residue = 4 * iota((8, lanes), 0) + member
    spot = iota((128, lanes), 0).astype(F32)
    aside = iota((sources, 128), 1) < 64

    def one_slot(i):
        pick = pl.ds(i, sources, stride=ROWS)
        low, high = facets_lo[pick, :], facets_hi[pick, :]
        mine = pltpu.roll(param[...], (320 - 16 * i) & 255, 1)[:, :128]
        blocks = [low, pltpu.roll(low, 64, 1), high, pltpu.roll(high, 64, 1)]
        turned = jnp.concatenate([jnp.where(aside, block, mine) for block in blocks], axis=0).T
        par = turned[64:80]
        block, turn_u, col = [par[k : k + 1].astype(jnp.int32) for k in (9, 10, 11)]
        row_r, row_i = power_of(
            par[0:1], par[3:4], (residue - turn_u) & 15, par[2:3], par[5:6]
        )
        one = jnp.ones((16, lanes), F32)
        col_r, col_i = power_of(
            par[1:2], par[4:5], (iota((16, lanes), 0) - col) & 15, one, one * 0.0
        )
        spots = (block + jnp.where(residue < turn_u, 1, 0) + 32 * member).astype(F32)
        ahead = iota((TW, lanes), 0) - col
        window = jnp.where((ahead & -16) == 0, 1.0, 0.0).astype(BF16)
        return turned, row_r, row_i, col_r, col_i, spots, window

    def one_column(j, carry):
        slots = [one_slot(CAP * j + k) for k in range(CAP)]
        for group in range(4):
            spreads, hots = [], []
            for turned, row_r, row_i, col_r, col_i, spots, window in slots:
                patch = turned[16 * group : 16 * group + 16]
                cos_p, sin_p = row_r[group : group + 1], row_i[group : group + 1]
                real = (patch * (cos_p * col_r - sin_p * col_i)).astype(BF16)
                imag = (patch * (cos_p * col_i + sin_p * col_r)).astype(BF16)
                spreads.append(
                    jnp.concatenate(
                        [jnp.concatenate([real] * 16, axis=0) * window]
                        + [jnp.concatenate([imag] * 16, axis=0) * window],
                        axis=0,
                    )
                )
                hots.append(
                    jnp.where(spot == spots[group : group + 1], 1.0, 0.0).astype(BF16)
                )
            spread = jnp.concatenate(spreads, axis=1)
            hot = jnp.concatenate(hots, axis=1)
            plane[:, 128 * group : 128 * group + 128] = mm(spread, hot, NT).astype(BF16)
        weight = reach_weight(mx, TW, float(REACH - j))
        total[...] += weight * mm(fblk_ref[...], plane[...])
        return carry

    for j in range(OFFSETS):
        one_column(j, 0)
    value = total[...].astype(BF16)
    value_ref[...] = value
    row_transform(value, grow_ref, out_ref)


def column_sums(incoming, fblk, grow):
    return pl.pallas_call(
        column_kernel,
        out_shape=(
            jax.ShapeDtypeStruct((2, TW, HALF), BF16),
            jax.ShapeDtypeStruct((2 * TW, TH), BF16),
        ),
        in_specs=[pl.BlockSpec(memory_space=pltpu.VMEM)] * 3,
        out_specs=tuple([pl.BlockSpec(memory_space=pltpu.VMEM)] * 2),
        scratch_shapes=[
            pltpu.VMEM((incoming.shape[0], 128), F32),
            pltpu.VMEM((incoming.shape[0], 128), F32),
            pltpu.VMEM((incoming.shape[0] // ROWS, 256), F32),
            pltpu.VMEM((2 * TW, TH), BF16),
            pltpu.VMEM((2 * TW, TH), F32),
        ],
        compiler_params=pltpu.CompilerParams(vmem_limit_bytes=20 << 20),
        cost_estimate=pl.CostEstimate(flops=6_000_000_000, bytes_accessed=3 << 20, transcendentals=40_000),
        name="column_sums",
    )(incoming, fblk, grow)


def second_kernel(value_ref, grow_ref, out_ref):
    row_transform(value_ref[...], grow_ref, out_ref)


def second_half(value, grow):
    return pl.pallas_call(
        second_kernel,
        out_shape=jax.ShapeDtypeStruct((2, TW, HALF), BF16),
        in_specs=[pl.BlockSpec(memory_space=pltpu.VMEM)] * 2,
        out_specs=pl.BlockSpec(memory_space=pltpu.VMEM),
        compiler_params=pltpu.CompilerParams(vmem_limit_bytes=8 << 20),
        cost_estimate=pl.CostEstimate(flops=600_000_000, bytes_accessed=2 << 20, transcendentals=0),
        name="second_half",
    )(value, grow)


def image_kernel(half, *refs):
    side = (1 - 2 * (lax.axis_index("narrow") & 1)).astype(F32)
    pieces = refs[:OFFSETS]
    hblk_ref, kr_ref, ki_ref = refs[OFFSETS : OFFSETS + 3]
    before, out_ref, band = refs[OFFSETS + 3 : -2], refs[-2], refs[-1]
    my = iota((1, HALF), 1) + HALF * half
    weights = [reach_weight(my, TH, side * float(REACH - at)) for at in range(OFFSETS)]
    for part in range(2):
        acc = None
        for weight, piece in zip(weights, pieces):
            term = weight * piece[part].astype(F32)
            acc = term if acc is None else acc + term
        band[TW * part : TW * part + TW, :] = acc.astype(BF16)
    image = mm(hblk_ref[...], band[...]).astype(BF16)
    image_r, image_i = image[:TW], image[TW:]
    real = (mm(kr_ref[...], image_r, NT) - mm(ki_ref[...], image_i, NT)) * SCALE
    imag = (mm(kr_ref[...], image_i, NT) + mm(ki_ref[...], image_r, NT)) * SCALE
    if before:
        real = real + before[0][0]
        imag = imag + before[0][1]
    out_ref[0] = real
    out_ref[1] = imag


def image_of(half, pieces, tables, before):
    operands = (*pieces, *tables, *before)
    return pl.pallas_call(
        functools.partial(image_kernel, half),
        out_shape=jax.ShapeDtypeStruct((2, TH, TW), F32),
        in_specs=[pl.BlockSpec(memory_space=pltpu.VMEM)] * len(operands),
        out_specs=pl.BlockSpec(memory_space=pltpu.VMEM),
        scratch_shapes=[pltpu.VMEM((2 * TW, HALF), BF16)],
        compiler_params=pltpu.CompilerParams(vmem_limit_bytes=16 << 20),
        cost_estimate=pl.CostEstimate(flops=900_000_000, bytes_accessed=4 << 20, transcendentals=0),
        name="image",
    )(*operands)


def swap(value, first):
    count = lax.axis_size("narrow")
    pairs = [(low, low + 1) for low in range(first, count - 1, 2)]
    return lax.ppermute(value, "narrow", pairs + [(high, low) for low, high in pairs])


def narrow_pieces(mine):
    above1 = swap(mine, 0)
    below1 = swap(mine, 1)
    above2 = swap(below1, 0)
    below2 = swap(above1, 1)
    return [below2, below1, mine, above1, above2]


def local(amplitude, tilt, owner, row_offset, col_offset):
    wide_count = lax.axis_size("wide")
    fblk, grow_a, grow_b, hblk, kr_a, ki_a, kr_b, ki_b = make_tables()
    outgoing = pack(amplitude, tilt, owner, row_offset, col_offset, wide_count)
    incoming = lax.all_to_all(
        outgoing.reshape(wide_count, ROWS, 256), "wide", split_axis=0, concat_axis=0, tiled=True
    ).reshape(wide_count * ROWS, 256)
    first, value = column_sums(incoming, fblk, grow_a)
    second = second_half(value, grow_b)
    partial = image_of(0, narrow_pieces(first), (hblk, kr_a, ki_a), ())
    return image_of(1, narrow_pieces(second), (hblk, kr_b, ki_b), (partial,))


def solution(mesh):
    in_specs = (
        P(("wide", "narrow"), None),
        P(None, ("wide", "narrow")),
        P(("wide", "narrow"), None),
        P(("wide", "narrow")),
        P(("wide", "narrow")),
    )
    out_specs = P(None, "narrow", "wide")
    return jax.shard_map(local, mesh=mesh, in_specs=in_specs, out_specs=out_specs, check_vma=False)
```

time: 98.3 us -> 92 us (0.936)
  starting transfers between devices: 56.4 us -> 50.1 us
  waiting for transfers between devices: 21 us -> 23.5 us
  local copies, waits for them, and re-layouts: 3.37 us -> 1.83 us
  Pallas kernels: 16.9 us -> 15.9 us
    ppermute x8, starting transfers between devices: 43.7 us -> 37.5 us  [swap(): lax.ppermute(value, 'narrow', pairs + [(high, low) for low, high in pairs])]
    ppermute x8, waiting for transfers between devices: 5.01 us -> 7.46 us  [swap(): lax.ppermute(value, 'narrow', pairs + [(high, low) for low, high in pairs])]
    pallas_call x3 -> x5, Pallas kernels: 14.7 us -> 12.9 us  [the longest x1 8.21 us: column_sums(): pl.pallas_call(column_kernel, out_shape=(jax.ShapeDtypeStruct((2, TW, HAL...]
    unnamed x14 -> x4, local copies, waits for them, and re-layouts: 3.37 us -> 1.83 us
  transfers between devices with their start and end apart: 9 -> 9, of which waited for: 3 -> 3; matrix products, arithmetic and copies ran while one was open for 0% -> 0% of each run, Pallas kernels for 2% -> 3%
where the time goes in v1:
time: 92 us; the launch traced here: 91.5 us
  starting transfers between devices  50.1 us (54%)
  waiting for transfers between devices  23.5 us (26%)
  Pallas kernels  15.9 us (17%)
  local copies, waits for them, and re-layouts  1.83 us (2%)
    ppermute x8, starting transfers between devices, swap(): lax.ppermute(value, 'narrow', pairs + [(high, low) for low, high in pairs])  37.5 us
    all_to_all x1, waiting for transfers between devices, local(): lax.all_to_all(outgoing.reshape(wide_count, ROWS, 256), 'wide', split_axi...  16 us
    all_to_all x1, starting transfers between devices, local(): lax.all_to_all(outgoing.reshape(wide_count, ROWS, 256), 'wide', split_axi...  12.6 us
    pallas_call x1, Pallas kernels, column_sums(): pl.pallas_call(column_kernel, out_shape=(jax.ShapeDtypeStruct((2, TW, HAL...  8.21 us
    ppermute x8, waiting for transfers between devices, swap(): lax.ppermute(value, 'narrow', pairs + [(high, low) for low, high in pairs])  7.46 us
    pallas_call x1, Pallas kernels, pack(): pl.pallas_call(pack_kernel, out_shape=jax.ShapeDtypeStruct((wide_count *...  3.08 us
    pallas_call x2, Pallas kernels, image_of(): pl.pallas_call(functools.partial(image_kernel, half), out_shape=jax.Shape...  2.73 us
  transfers between devices with their start and end apart: 9, of which 3 were waited for; matrix products, arithmetic and copies ran while one was open for 0% of the time, Pallas kernels for 3%

profile of v1, /device:TPU:22, one launch (start us, length us, event | category | flops | bytes accessed | tf_op | source)
XLA Modules:
  0.0 91.5 jit_solution(9650589431694513060)
XLA Ops:
  0.0 3.1 %pack.1 = bf16[1024,256]{1,0:T(8,128)(2,1)} custom-call(f32[64,256]{1,0:T(8,128)} %amp_ref.1, f32[3,64]{1,0:T(4,128)} %tilt_ref.1, s32[1,64]{1,0:T(1,128)} %bitcast.7, s32[1,64]{1,0:T(1,128)} %bitcast.8, s32[1,64]{1,0:T(1,128)} %bitcast.9), custom_call_target="tpu_custom_call" | custom-call | tf_op jit(solution)/shard_map/pack/pallas_call | solution.py:173
  3.1 12.6 %all-to-all-start = ((bf16[64,16,256]{2,1,0:T(8,128)(2,1)}), bf16[64,16,256]{2,1,0:T(8,128)(2,1)S(1)}, u32[]{:S(2)}, u32[]{:S(2)}) async-start(bf16[64,16,256]{2,1,0:T(8,128)(2,1)} %bitcast.6), calls=%async_computation | async-start | bytes 1048576 | tf_op jit(solution)/shard_map/all_to_all | solution.py:373
  15.7 1.5 %tables.1 = (bf16[512,512]{1,0:T(8,128)(2,1)S(1)}, bf16[512,512]{1,0:T(8,128)(2,1)S(1)}, bf16[512,512]{1,0:T(8,128)(2,1)S(1)}, bf16[512,512]{1,0:T(8,128)(2,1)S(...) custom-call(), custom_call_target="tpu_custom_call" | custom-call | flops 8000000 | bytes 3145728 | tf_op jit(solution)/shard_map/tables/pallas_call | solution.py:107
  17.2 0.0 copy-start
  17.2 0.8 copy-done
  18.0 16.0 %all-to-all-done = bf16[64,16,256]{2,1,0:T(8,128)(2,1)S(1)} async-done(((bf16[64,16,256]{2,1,0:T(8,128)(2,1)}), bf16[64,16,256]{2,1,0:T(8,128)(2,1)S(1)}, u32[]{:S(2)}, u32[]{:S(2)}) %all-to-all-start) | async-done | bytes 524320 | tf_op jit(solution)/shard_map/all_to_all | solution.py:373
  34.0 0.0 copy-start.1
  34.0 1.0 %copy-done.1 = bf16[512,512]{1,0:T(8,128)(2,1)S(1)} copy-done((bf16[512,512]{1,0:T(8,128)(2,1)S(1)}, bf16[512,512]{1,0:T(8,128)(2,1)}, u32[]{:S(2)}) %copy-start.1) | copy-done | bytes 524312
  35.1 8.2 %column_sums.1 = (bf16[2,256,256]{2,1,0:T(8,128)(2,1)S(1)}, bf16[512,512]{1,0:T(8,128)(2,1)S(1)}) custom-call(bf16[1024,256]{1,0:T(8,128)(2,1)S(1)} %bitcast.5, bf16[512,512]{1,0:T(8,128)(2,1)S(1)} %get-tuple-element.15.fblk_ref, bf16[512,512]{1,0:T(8,128)(2,1)S(1)} %copy-done.1), custom_call_target="tpu_custom_call" | custom-call | flops 6000000000 | bytes 3145728 | tf_op jit(solution)/shard_map/column_sums/pallas_call | solution.py:280
  43.3 5.2 %collective-permute-start.4 = (bf16[2,256,256]{2,1,0:T(8,128)(2,1)S(1)}, bf16[2,256,256]{2,1,0:T(8,128)(2,1)S(1)}, u32[]{:S(2)}, u32[]{:S(2)}) collective-permute-start(bf16[2,256,256]{2,1,0:T(8,128)(2,1)S(1)} %get-tuple-element.22.refs_2_), channel_id=1, source_target_pairs={{0,1},{2,3},{4,5},{6,7},{8,9},{10,11},{12,13},{14,15},{1,0},{3,2},... | collective-permute-start | bytes 786440 | tf_op jit(solution)/shard_map/ppermute | solution.py:358
  48.5 14.7 %collective-permute-start.6 = (bf16[2,256,256]{2,1,0:T(8,128)(2,1)S(1)}, bf16[2,256,256]{2,1,0:T(8,128)(2,1)S(1)}, u32[]{:S(2)}, u32[]{:S(2)}) collective-permute-start(bf16[2,256,256]{2,1,0:T(8,128)(2,1)S(1)} %get-tuple-element.22.refs_2_), channel_id=1, source_target_pairs={{1,2},{3,4},{5,6},{7,8},{9,10},{11,12},{13,14},{2,1},{4,3},{6,5},{... | collective-permute-start | bytes 786440 | tf_op jit(solution)/shard_map/ppermute | solution.py:358
  63.2 0.4 second_half.1.refs_2_
  63.6 1.9 %collective-permute-start = (bf16[2,256,256]{2,1,0:T(8,128)(2,1)S(1)}, bf16[2,256,256]{2,1,0:T(8,128)(2,1)S(1)}, u32[]{:S(2)}, u32[]{:S(2)}) collective-permute-start(bf16[2,256,256]{2,1,0:T(8,128)(2,1)S(1)} %second_half.1.refs_2_), channel_id=1, source_target_pairs={{0,1},{2,3},{4,5},{6,7},{8,9},{10,11},{12,13},{14,15},{1,0},{3,2},... | collective-permute-start | bytes 786440 | tf_op jit(solution)/shard_map/ppermute | solution.py:358
  65.5 3.9 %collective-permute-start.2 = (bf16[2,256,256]{2,1,0:T(8,128)(2,1)S(1)}, bf16[2,256,256]{2,1,0:T(8,128)(2,1)S(1)}, u32[]{:S(2)}, u32[]{:S(2)}) collective-permute-start(bf16[2,256,256]{2,1,0:T(8,128)(2,1)S(1)} %second_half.1.refs_2_), channel_id=1, source_target_pairs={{1,2},{3,4},{5,6},{7,8},{9,10},{11,12},{13,14},{2,1},{4,3},{6,5},{... | collective-permute-start | bytes 786440 | tf_op jit(solution)/shard_map/ppermute | solution.py:358
  69.5 0.0 collective-permute-done.4.refs_3_
  69.5 4.0 %collective-permute-start.5 = (bf16[2,256,256]{2,1,0:T(8,128)(2,1)S(1)}, bf16[2,256,256]{2,1,0:T(8,128)(2,1)S(1)}, u32[]{:S(2)}, u32[]{:S(2)}) collective-permute-start(bf16[2,256,256]{2,1,0:T(8,128)(2,1)S(1)} %collective-permute-done.4.refs_3_), channel_id=1, source_target_pairs={{1,2},{3,4},{5,6},{7,8},{9,10},{11,12},{13,14},{2,1},{4,3},{6,5},{... | collective-permute-start | bytes 786440 | tf_op jit(solution)/shard_map/ppermute | solution.py:358
  73.5 0.0 collective-permute-done.6.refs_1_
  73.5 1.9 %collective-permute-start.7 = (bf16[2,256,256]{2,1,0:T(8,128)(2,1)S(1)}, bf16[2,256,256]{2,1,0:T(8,128)(2,1)S(1)}, u32[]{:S(2)}, u32[]{:S(2)}) collective-permute-start(bf16[2,256,256]{2,1,0:T(8,128)(2,1)S(1)} %collective-permute-done.6.refs_1_), channel_id=1, source_target_pairs={{0,1},{2,3},{4,5},{6,7},{8,9},{10,11},{12,13},{14,15},{1,0},{3,2},... | collective-permute-start | bytes 786440 | tf_op jit(solution)/shard_map/ppermute | solution.py:358
  75.5 0.0 collective-permute-done.refs_3_
  75.5 3.9 %collective-permute-start.1 = (bf16[2,256,256]{2,1,0:T(8,128)(2,1)S(1)}, bf16[2,256,256]{2,1,0:T(8,128)(2,1)S(1)}, u32[]{:S(2)}, u32[]{:S(2)}) collective-permute-start(bf16[2,256,256]{2,1,0:T(8,128)(2,1)S(1)} %collective-permute-done.refs_3_), channel_id=1, source_target_pairs={{1,2},{3,4},{5,6},{7,8},{9,10},{11,12},{13,14},{2,1},{4,3},{6,5},{... | collective-permute-start | bytes 786440 | tf_op jit(solution)/shard_map/ppermute | solution.py:358
  79.4 0.0 collective-permute-done.2.refs_1_
  79.4 1.9 %collective-permute-start.3 = (bf16[2,256,256]{2,1,0:T(8,128)(2,1)S(1)}, bf16[2,256,256]{2,1,0:T(8,128)(2,1)S(1)}, u32[]{:S(2)}, u32[]{:S(2)}) collective-permute-start(bf16[2,256,256]{2,1,0:T(8,128)(2,1)S(1)} %collective-permute-done.2.refs_1_), channel_id=1, source_target_pairs={{0,1},{2,3},{4,5},{6,7},{8,9},{10,11},{12,13},{14,15},{1,0},{3,2},... | collective-permute-start | bytes 786440 | tf_op jit(solution)/shard_map/ppermute | solution.py:358
  81.3 3.0 %collective-permute-done.5.refs_0_ = bf16[2,256,256]{2,1,0:T(8,128)(2,1)S(1)} collective-permute-done((bf16[2,256,256]{2,1,0:T(8,128)(2,1)S(1)}, bf16[2,256,256]{2,1,0:T(8,128)(2,1)S(1)}, u32[]{:S(2)}, u32[]{:S(2)}) %collective-permute-start.5) | collective-permute-done | bytes 262176 | tf_op jit(solution)/shard_map/ppermute | solution.py:358
  84.3 0.0 collective-permute-done.7.refs_4_
  84.4 0.9 image.2.refs_8_
  85.2 4.4 %collective-permute-done.1.refs_0_ = bf16[2,256,256]{2,1,0:T(8,128)(2,1)S(1)} collective-permute-done((bf16[2,256,256]{2,1,0:T(8,128)(2,1)S(1)}, bf16[2,256,256]{2,1,0:T(8,128)(2,1)S(1)}, u32[]{:S(2)}, u32[]{:S(2)}) %collective-permute-start.1) | collective-permute-done | bytes 262176 | tf_op jit(solution)/shard_map/ppermute | solution.py:358
  89.7 0.0 collective-permute-done.3.refs_4_
  89.7 1.8 %image.3 = f32[2,512,256]{2,1,0:T(8,128)} custom-call(bf16[2,256,256]{2,1,0:T(8,128)(2,1)S(1)} %collective-permute-done.1.refs_0_, bf16[2,256,256]{2,1,0:T(8,128)(2,1)S(1)} %collective-permute-done.2.refs_1_, bf16[2,256,256]{2,1,0:T(8,128)(2,1)S(1)} %second_half.1.refs_2_, bf16[2,256,256]{2,1,0:T(8,128)(2,1)S(1)} %collective-permute-done.refs_3_, ...), custom_call_target="tpu_custom_call" | custom-call | flops 900000000 | bytes 4194304 | tf_op jit(solution)/shard_map/image/pallas_call | solution.py:343
Async XLA Ops:
  3.1 30.9 %all-to-all-start = ((bf16[64,16,256]{2,1,0:T(8,128)(2,1)}), bf16[64,16,256]{2,1,0:T(8,128)(2,1)S(1)}, u32[]{:S(2)}, u32[]{:S(2)}) async-start(bf16[64,16,256]{2,1,0:T(8,128)(2,1)} %bitcast.6), calls=%async_computation | async-start | bytes 1048576 | tf_op jit(solution)/shard_map/all_to_all | solution.py:373
  17.2 0.8 copy-start
  34.0 1.0 %copy-start.1 = (bf16[512,512]{1,0:T(8,128)(2,1)S(1)}, bf16[512,512]{1,0:T(8,128)(2,1)}, u32[]{:S(2)}) copy-start(bf16[512,512]{1,0:T(8,128)(2,1)} %copy-done) | copy-start | bytes 1572868
  43.3 26.2 %collective-permute-start.4 = (bf16[2,256,256]{2,1,0:T(8,128)(2,1)S(1)}, bf16[2,256,256]{2,1,0:T(8,128)(2,1)S(1)}, u32[]{:S(2)}, u32[]{:S(2)}) collective-permute-start(bf16[2,256,256]{2,1,0:T(8,128)(2,1)S(1)} %get-tuple-element.22.refs_2_), channel_id=1, source_target_pairs={{0,1},{2,3},{4,5},{6,7},{8,9},{10,11},{12,13},{14,15},{1,0},{3,2},... | collective-permute-start | bytes 786440 | tf_op jit(solution)/shard_map/ppermute | solution.py:358
  48.5 25.1 %collective-permute-start.6 = (bf16[2,256,256]{2,1,0:T(8,128)(2,1)S(1)}, bf16[2,256,256]{2,1,0:T(8,128)(2,1)S(1)}, u32[]{:S(2)}, u32[]{:S(2)}) collective-permute-start(bf16[2,256,256]{2,1,0:T(8,128)(2,1)S(1)} %get-tuple-element.22.refs_2_), channel_id=1, source_target_pairs={{1,2},{3,4},{5,6},{7,8},{9,10},{11,12},{13,14},{2,1},{4,3},{6,5},{... | collective-permute-start | bytes 786440 | tf_op jit(solution)/shard_map/ppermute | solution.py:358
  63.6 11.8 %collective-permute-start = (bf16[2,256,256]{2,1,0:T(8,128)(2,1)S(1)}, bf16[2,256,256]{2,1,0:T(8,128)(2,1)S(1)}, u32[]{:S(2)}, u32[]{:S(2)}) collective-permute-start(bf16[2,256,256]{2,1,0:T(8,128)(2,1)S(1)} %second_half.1.refs_2_), channel_id=1, source_target_pairs={{0,1},{2,3},{4,5},{6,7},{8,9},{10,11},{12,13},{14,15},{1,0},{3,2},... | collective-permute-start | bytes 786440 | tf_op jit(solution)/shard_map/ppermute | solution.py:358
  65.5 13.9 %collective-permute-start.2 = (bf16[2,256,256]{2,1,0:T(8,128)(2,1)S(1)}, bf16[2,256,256]{2,1,0:T(8,128)(2,1)S(1)}, u32[]{:S(2)}, u32[]{:S(2)}) collective-permute-start(bf16[2,256,256]{2,1,0:T(8,128)(2,1)S(1)} %second_half.1.refs_2_), channel_id=1, source_target_pairs={{1,2},{3,4},{5,6},{7,8},{9,10},{11,12},{13,14},{2,1},{4,3},{6,5},{... | collective-permute-start | bytes 786440 | tf_op jit(solution)/shard_map/ppermute | solution.py:358
  69.5 14.9 %collective-permute-start.5 = (bf16[2,256,256]{2,1,0:T(8,128)(2,1)S(1)}, bf16[2,256,256]{2,1,0:T(8,128)(2,1)S(1)}, u32[]{:S(2)}, u32[]{:S(2)}) collective-permute-start(bf16[2,256,256]{2,1,0:T(8,128)(2,1)S(1)} %collective-permute-done.4.refs_3_), channel_id=1, source_target_pairs={{1,2},{3,4},{5,6},{7,8},{9,10},{11,12},{13,14},{2,1},{4,3},{6,5},{... | collective-permute-start | bytes 786440 | tf_op jit(solution)/shard_map/ppermute | solution.py:358
  73.5 10.8 %collective-permute-start.7 = (bf16[2,256,256]{2,1,0:T(8,128)(2,1)S(1)}, bf16[2,256,256]{2,1,0:T(8,128)(2,1)S(1)}, u32[]{:S(2)}, u32[]{:S(2)}) collective-permute-start(bf16[2,256,256]{2,1,0:T(8,128)(2,1)S(1)} %collective-permute-done.6.refs_1_), channel_id=1, source_target_pairs={{0,1},{2,3},{4,5},{6,7},{8,9},{10,11},{12,13},{14,15},{1,0},{3,2},... | collective-permute-start | bytes 786440 | tf_op jit(solution)/shard_map/ppermute | solution.py:358
  75.5 14.2 %collective-permute-start.1 = (bf16[2,256,256]{2,1,0:T(8,128)(2,1)S(1)}, bf16[2,256,256]{2,1,0:T(8,128)(2,1)S(1)}, u32[]{:S(2)}, u32[]{:S(2)}) collective-permute-start(bf16[2,256,256]{2,1,0:T(8,128)(2,1)S(1)} %collective-permute-done.refs_3_), channel_id=1, source_target_pairs={{1,2},{3,4},{5,6},{7,8},{9,10},{11,12},{13,14},{2,1},{4,3},{6,5},{... | collective-permute-start | bytes 786440 | tf_op jit(solution)/shard_map/ppermute | solution.py:358
  79.4 10.3 %collective-permute-start.3 = (bf16[2,256,256]{2,1,0:T(8,128)(2,1)S(1)}, bf16[2,256,256]{2,1,0:T(8,128)(2,1)S(1)}, u32[]{:S(2)}, u32[]{:S(2)}) collective-permute-start(bf16[2,256,256]{2,1,0:T(8,128)(2,1)S(1)} %collective-permute-done.2.refs_1_), channel_id=1, source_target_pairs={{0,1},{2,3},{4,5},{6,7},{8,9},{10,11},{12,13},{14,15},{1,0},{3,2},... | collective-permute-start | bytes 786440 | tf_op jit(solution)/shard_map/ppermute | solution.py:358

commit v2 on v1

--- a/solution.py
+++ b/solution.py
@@ -17,6 +17,7 @@
 CAP = 3
 SLOTS = OFFSETS * CAP
 HALF = TH // 2
+PARTS = 4
 ROWS = 16
 SPREAD = 16.0
 SCALE = 1.0 / math.sqrt(TH * TW)
@@ -58,7 +59,8 @@
     return ((a * b) & (length - 1)).astype(F32) * (2.0 * math.pi / length)
 
 
-def table_kernel(fblk_ref, grow_a_ref, grow_b_ref, hblk_ref, kr_a_ref, ki_a_ref, kr_b_ref, ki_b_ref):
+def table_kernel(lead_ref, grow_b_ref, hblk_ref, kr_a_ref, ki_a_ref, kr_b_ref, ki_b_ref):
+    fblk_ref, grow_a_ref = lead_ref.at[:TH], lead_ref.at[TH:]
     fine_r, fine_i = cis(-turn_angle(iota((16, TW), 0), iota((16, TW), 1), TW))
     wide_r, wide_i = cis(-turn_angle(iota((16, TW), 0), iota((16, TW), 1), 16))
     for a in range(16):
@@ -106,20 +108,44 @@
     half = jax.ShapeDtypeStruct((TH, HALF), BF16)
     return pl.pallas_call(
         table_kernel,
-        out_shape=(square, square, square, square, half, half, half, half),
-        out_specs=tuple([pl.BlockSpec(memory_space=pltpu.VMEM)] * 8),
+        out_shape=(jax.ShapeDtypeStruct((2 * TH, TH), BF16), square, square, half, half, half, half),
+        out_specs=tuple([pl.BlockSpec(memory_space=pltpu.VMEM)] * 7),
         compiler_params=pltpu.CompilerParams(vmem_limit_bytes=12 << 20),
         cost_estimate=pl.CostEstimate(flops=8_000_000, bytes_accessed=3 << 20, transcendentals=200_000),
         name="tables",
     )()
 
 
-def pack_kernel(amp_ref, tilt_ref, owner_ref, row_ref, col_ref, out_ref):
+def pack_kernel(amp_at, tilt_at, owner_at, row_at, col_at, out_at, *scratch):
+    amp_ref, tilt_ref, owner_ref, row_ref, col_ref, out_ref, sems, out_sems = scratch
+    copies = [
+        pltpu.make_async_copy(place, ref, sems.at[k])
+        for k, (place, ref) in enumerate(
+            (
+                (owner_at, owner_ref),
+                (row_at, row_ref),
+                (col_at, col_ref),
+                (tilt_at, tilt_ref),
+                (amp_at, amp_ref),
+            )
+        )
+    ]
+    for copy in copies:
+        copy.start()
     count = amp_ref.shape[0]
     total = out_ref.shape[0]
+    sub, lane = iota((count, count), 0), iota((count, count), 1)
+    at = iota((total, count), 0)
+    wanted = CAP * (at >> 4) + (at & 15) - CAP * REACH
+    wanted = jnp.where((at & 15) == SLOTS, -1, wanted).astype(F32)
+    old = iota((256, 256), 0)
+    new = ((old >> 4) & 3) * 64 + (old >> 6) * 16 + (old & 15)
+    order = jnp.where(iota((256, 256), 1) == new, 1.0, 0.0).astype(BF16)
+    repeat = jnp.where((iota((16, 256), 1) & 15) == iota((16, 256), 0), 1.0, 0.0).astype(BF16)
+    for copy in copies:
+        copy.wait()
     row, col = row_ref[...], col_ref[...]
     owner = owner_ref[...].astype(F32)
-    sub, lane = iota((count, count), 0), iota((count, count), 1)
 
     def upright(vector):
         picked = jnp.where(sub == lane, vector.astype(F32), 0.0)
@@ -128,6 +154,7 @@
     same = (upright(owner) == owner) & (sub < lane)
     rank = jnp.sum(jnp.where(same, 1.0, 0.0), axis=0, keepdims=True)
     key = CAP * owner + rank
+    chosen = jnp.where(wanted == key, 1.0, 0.0).astype(BF16)
     amp = amp_ref[...]
     turn_v = upright(col & 15).astype(jnp.int32)
     turn_u = upright(row & 15).astype(jnp.int32)
@@ -139,14 +166,7 @@
         amp = jnp.where((turn_v & step) != 0, moved, amp)
     for step in (1, 2, 4, 8):
         amp = jnp.where((turn_u & step) != 0, pltpu.roll(amp, 16 * step, 1), amp)
-    at = iota((total, count), 0)
-    wanted = CAP * (at >> 4) + (at & 15) - CAP * REACH
-    wanted = jnp.where((at & 15) == SLOTS, -1, wanted).astype(F32)
-    chosen = jnp.where(wanted == key, 1.0, 0.0).astype(BF16)
-    old = iota((256, 256), 0)
-    new = ((old >> 4) & 3) * 64 + (old >> 6) * 16 + (old & 15)
-    order = jnp.where(iota((256, 256), 1) == new, 1.0, 0.0).astype(BF16)
-    placed = mm(chosen, mm(amp.astype(BF16), order).astype(BF16))
+    amp = mm(amp.astype(BF16), order).astype(BF16)
     tilt = tilt_ref[...]
     high = tilt.astype(BF16).astype(F32)
     middle = (tilt - high).astype(BF16).astype(F32)
@@ -157,15 +177,26 @@
     extras = jnp.zeros((16, count), F32)
     for k, line in enumerate(lines):
         extras = jnp.where(entry == k, line, extras)
-    mine = mm(chosen, extras.astype(BF16), NT)
-    repeat = jnp.where((iota((16, 256), 1) & 15) == iota((16, 256), 0), 1.0, 0.0).astype(BF16)
-    mine = mm(mine.astype(BF16), repeat)
-    here = iota((total, 256), 0) & 15
-    mine = jnp.where((iota((total, 256), 1) >> 4) == here, mine, 0.0)
-    mine = jnp.sum(mine.reshape(total // ROWS, ROWS, 256), axis=1, keepdims=True)
-    placed = placed.reshape(total // ROWS, ROWS, 256)
-    result = jnp.where(iota(placed.shape, 1) == SLOTS, mine, placed)
-    out_ref[...] = result.reshape(total, 256).astype(BF16)
+    extras = lax.dot_general(
+        extras.astype(BF16), repeat, (((0,), (0,)), ((), ())), preferred_element_type=F32
+    ).astype(BF16)
+    both = jnp.concatenate([amp, extras], axis=1)
+    part = total // PARTS
+    keep = (iota((part, 256), 1) >> 4) == (iota((part, 256), 0) & 15)
+    last = iota((part // ROWS, ROWS, 256), 1) == SLOTS
+    sends = []
+    for k in range(PARTS):
+        rows = pl.ds(part * k, part)
+        found = mm(chosen[part * k : part * k + part], both)
+        placed = found[:, :256].reshape(part // ROWS, ROWS, 256)
+        mine = jnp.where(keep, found[:, 256:], 0.0).reshape(part // ROWS, ROWS, 256)
+        mine = jnp.sum(mine, axis=1, keepdims=True)
+        out_ref[rows, :] = jnp.where(last, mine, placed).reshape(part, 256).astype(BF16)
+        send = pltpu.make_async_copy(out_ref.at[rows], out_at.at[rows], out_sems.at[k])
+        send.start()
+        sends.append(send)
+    for send in sends:
+        send.wait()
 
 
 def pack(amplitude, tilt, owner, row_offset, col_offset, wide_count):
@@ -173,8 +204,18 @@
     return pl.pallas_call(
         pack_kernel,
         out_shape=jax.ShapeDtypeStruct((wide_count * ROWS, 256), BF16),
-        in_specs=[pl.BlockSpec(memory_space=pltpu.VMEM)] * 5,
-        out_specs=pl.BlockSpec(memory_space=pltpu.VMEM),
+        in_specs=[pl.BlockSpec(memory_space=pl.ANY)] * 5,
+        out_specs=pl.BlockSpec(memory_space=pl.ANY),
+        scratch_shapes=[
+            pltpu.VMEM((count, 256), F32),
+            pltpu.VMEM((3, count), F32),
+            pltpu.VMEM((1, count), jnp.int32),
+            pltpu.VMEM((1, count), jnp.int32),
+            pltpu.VMEM((1, count), jnp.int32),
+            pltpu.VMEM((wide_count * ROWS, 256), BF16),
+            pltpu.SemaphoreType.DMA((5,)),
+            pltpu.SemaphoreType.DMA((PARTS,)),
+        ],
         compiler_params=pltpu.CompilerParams(vmem_limit_bytes=63 << 20),
         name="pack",
     )(
@@ -204,7 +245,8 @@
     out_ref[1] = ((product[:TW, HALF:] + product[TW:, :HALF]) * SCALE).astype(BF16)
 
 
-def column_kernel(inc_ref, fblk_ref, grow_ref, out_ref, value_ref, facets_lo, facets_hi, param, plane, total):
+def column_kernel(inc_ref, lead_ref, out_ref, value_ref, facets_lo, facets_hi, param, plane, total):
+    fblk_ref, grow_ref = lead_ref.at[:TH], lead_ref.at[TH:]
     sources = inc_ref.shape[0] // ROWS
     lanes = 4 * sources
     facets_lo[...] = inc_ref[:, :128].astype(F32)
@@ -276,14 +318,14 @@
     row_transform(value, grow_ref, out_ref)
 
 
-def column_sums(incoming, fblk, grow):
+def column_sums(incoming, lead):
     return pl.pallas_call(
         column_kernel,
         out_shape=(
             jax.ShapeDtypeStruct((2, TW, HALF), BF16),
             jax.ShapeDtypeStruct((2 * TW, TH), BF16),
         ),
-        in_specs=[pl.BlockSpec(memory_space=pltpu.VMEM)] * 3,
+        in_specs=[pl.BlockSpec(memory_space=pltpu.VMEM)] * 2,
         out_specs=tuple([pl.BlockSpec(memory_space=pltpu.VMEM)] * 2),
         scratch_shapes=[
             pltpu.VMEM((incoming.shape[0], 128), F32),
@@ -295,7 +337,7 @@
         compiler_params=pltpu.CompilerParams(vmem_limit_bytes=20 << 20),
         cost_estimate=pl.CostEstimate(flops=6_000_000_000, bytes_accessed=3 << 20, transcendentals=40_000),
         name="column_sums",
-    )(incoming, fblk, grow)
+    )(incoming, lead)
 
 
 def second_kernel(value_ref, grow_ref, out_ref):
@@ -318,34 +360,55 @@
     side = (1 - 2 * (lax.axis_index("narrow") & 1)).astype(F32)
     pieces = refs[:OFFSETS]
     hblk_ref, kr_ref, ki_ref = refs[OFFSETS : OFFSETS + 3]
-    before, out_ref, band = refs[OFFSETS + 3 : -2], refs[-2], refs[-1]
     my = iota((1, HALF), 1) + HALF * half
     weights = [reach_weight(my, TH, side * float(REACH - at)) for at in range(OFFSETS)]
-    for part in range(2):
+
+    def band(part):
         acc = None
         for weight, piece in zip(weights, pieces):
             term = weight * piece[part].astype(F32)
             acc = term if acc is None else acc + term
-        band[TW * part : TW * part + TW, :] = acc.astype(BF16)
-    image = mm(hblk_ref[...], band[...]).astype(BF16)
+        return acc.astype(BF16)
+
+    image = mm(hblk_ref[...], jnp.concatenate([band(0), band(1)], axis=0)).astype(BF16)
     image_r, image_i = image[:TW], image[TW:]
-    real = (mm(kr_ref[...], image_r, NT) - mm(ki_ref[...], image_i, NT)) * SCALE
-    imag = (mm(kr_ref[...], image_i, NT) + mm(ki_ref[...], image_r, NT)) * SCALE
-    if before:
-        real = real + before[0][0]
-        imag = imag + before[0][1]
-    out_ref[0] = real
-    out_ref[1] = imag
+
+    def share(rows, part):
+        kr, ki = kr_ref[rows, :], ki_ref[rows, :]
+        if part == 0:
+            return (mm(kr, image_r, NT) - mm(ki, image_i, NT)) * SCALE
+        return (mm(kr, image_i, NT) + mm(ki, image_r, NT)) * SCALE
+
+    if half == 0:
+        out_ref = refs[OFFSETS + 3]
+        for part in range(2):
+            out_ref[part] = share(pl.ds(0, TH), part)
+        return
+    before, out_at, out_ref, sems = refs[OFFSETS + 3 :]
+    sends = []
+    step = TH // 2
+    for k in range(4):
+        part, rows = k // 2, pl.ds(step * (k % 2), step)
+        out_ref[part, rows, :] = share(rows, part) + before[part, rows, :]
+        send = pltpu.make_async_copy(
+            out_ref.at[part, rows], out_at.at[part, rows], sems.at[k]
+        )
+        send.start()
+        sends.append(send)
+    for send in sends:
+        send.wait()
 
 
 def image_of(half, pieces, tables, before):
     operands = (*pieces, *tables, *before)
+    place = pl.ANY if half else pltpu.VMEM
+    scratch = [pltpu.VMEM((2, TH, TW), F32), pltpu.SemaphoreType.DMA((4,))] if half else []
     return pl.pallas_call(
         functools.partial(image_kernel, half),
         out_shape=jax.ShapeDtypeStruct((2, TH, TW), F32),
         in_specs=[pl.BlockSpec(memory_space=pltpu.VMEM)] * len(operands),
-        out_specs=pl.BlockSpec(memory_space=pltpu.VMEM),
-        scratch_shapes=[pltpu.VMEM((2 * TW, HALF), BF16)],
+        out_specs=pl.BlockSpec(memory_space=place),
+        scratch_shapes=scratch,
         compiler_params=pltpu.CompilerParams(vmem_limit_bytes=16 << 20),
         cost_estimate=pl.CostEstimate(flops=900_000_000, bytes_accessed=4 << 20, transcendentals=0),
         name="image",
@@ -368,12 +431,12 @@
 
 def local(amplitude, tilt, owner, row_offset, col_offset):
     wide_count = lax.axis_size("wide")
-    fblk, grow_a, grow_b, hblk, kr_a, ki_a, kr_b, ki_b = make_tables()
+    lead, grow_b, hblk, kr_a, ki_a, kr_b, ki_b = make_tables()
     outgoing = pack(amplitude, tilt, owner, row_offset, col_offset, wide_count)
     incoming = lax.all_to_all(
         outgoing.reshape(wide_count, ROWS, 256), "wide", split_axis=0, concat_axis=0, tiled=True
     ).reshape(wide_count * ROWS, 256)
-    first, value = column_sums(incoming, fblk, grow_a)
+    first, value = column_sums(incoming, lead)
     second = second_half(value, grow_b)
     partial = image_of(0, narrow_pieces(first), (hblk, kr_a, ki_a), ())
     return image_of(1, narrow_pieces(second), (hblk, kr_b, ki_b), (partial,))

time: 92 us -> 90.6 us (0.985)
  local copies, waits for them, and re-layouts: 1.83 us -> 0.79 us
    unnamed x4, local copies, waits for them, and re-layouts: 1.83 us -> 0.79 us
where the time goes in v2:
time: 90.6 us; the launch traced here: 90.2 us
  starting transfers between devices  50.2 us (55%)
  waiting for transfers between devices  23.5 us (26%)
  Pallas kernels  15.6 us (17%)
    ppermute x8, starting transfers between devices, swap(): lax.ppermute(value, 'narrow', pairs + [(high, low) for low, high in pairs])  37.5 us
    all_to_all x1, waiting for transfers between devices, local(): lax.all_to_all(outgoing.reshape(wide_count, ROWS, 256), 'wide', split_axi...  16 us
    all_to_all x1, starting transfers between devices, local(): lax.all_to_all(outgoing.reshape(wide_count, ROWS, 256), 'wide', split_axi...  12.6 us
    pallas_call x1, Pallas kernels, column_sums(): pl.pallas_call(column_kernel, out_shape=(jax.ShapeDtypeStruct((2, TW, HAL...  8.21 us
    ppermute x8, waiting for transfers between devices, swap(): lax.ppermute(value, 'narrow', pairs + [(high, low) for low, high in pairs])  7.47 us
    pallas_call x1, Pallas kernels, pack(): pl.pallas_call(pack_kernel, out_shape=jax.ShapeDtypeStruct((wide_count *...  2.76 us
    pallas_call x2, Pallas kernels, image_of(): pl.pallas_call(functools.partial(image_kernel, half), out_shape=jax.Shape...  2.67 us
  transfers between devices with their start and end apart: 9, of which 3 were waited for; matrix products, arithmetic and copies ran while one was open for 0% of the time, Pallas kernels for 3%

profile of v2, /device:TPU:22, one launch (start us, length us, event | category | flops | bytes accessed | tf_op | source)
XLA Modules:
  0.0 90.2 jit_solution(16666988942858967897)
XLA Ops:
  0.0 2.8 %pack.1 = bf16[1024,256]{1,0:T(8,128)(2,1)} custom-call(f32[64,256]{1,0:T(8,128)} %amp_at.1, f32[3,64]{1,0:T(4,128)} %tilt_at.1, s32[1,64]{1,0:T(1,128)} %bitcast.7, s32[1,64]{1,0:T(1,128)} %bitcast.8, s32[1,64]{1,0:T(1,128)} %bitcast.9), custom_call_target="tpu_custom_call" | custom-call | tf_op jit(solution)/shard_map/pack/pallas_call | solution.py:204
  2.8 12.6 %all-to-all-start = ((bf16[64,16,256]{2,1,0:T(8,128)(2,1)}), bf16[64,16,256]{2,1,0:T(8,128)(2,1)S(1)}, u32[]{:S(2)}, u32[]{:S(2)}) async-start(bf16[64,16,256]{2,1,0:T(8,128)(2,1)} %bitcast.6), calls=%async_computation | async-start | bytes 1048576 | tf_op jit(solution)/shard_map/all_to_all | solution.py:436
  15.4 1.5 %tables.1 = (bf16[1024,512]{1,0:T(8,128)(2,1)S(1)}, bf16[512,512]{1,0:T(8,128)(2,1)S(1)}, bf16[512,512]{1,0:T(8,128)(2,1)S(1)}, bf16[512,256]{1,0:T(8,128)(2,1)S...) custom-call(), custom_call_target="tpu_custom_call" | custom-call | flops 8000000 | bytes 3145728 | tf_op jit(solution)/shard_map/tables/pallas_call | solution.py:109
  16.9 0.0 copy-start
  16.9 0.8 copy-done
  17.7 16.0 %all-to-all-done = bf16[64,16,256]{2,1,0:T(8,128)(2,1)S(1)} async-done(((bf16[64,16,256]{2,1,0:T(8,128)(2,1)}), bf16[64,16,256]{2,1,0:T(8,128)(2,1)S(1)}, u32[]{:S(2)}, u32[]{:S(2)}) %all-to-all-start) | async-done | bytes 524320 | tf_op jit(solution)/shard_map/all_to_all | solution.py:436
  33.7 0.0 copy-start.1
  33.7 8.2 %column_sums.1 = (bf16[2,256,256]{2,1,0:T(8,128)(2,1)S(1)}, bf16[512,512]{1,0:T(8,128)(2,1)S(1)}) custom-call(bf16[1024,256]{1,0:T(8,128)(2,1)S(1)} %bitcast.5, bf16[1024,512]{1,0:T(8,128)(2,1)S(1)} %get-tuple-element.14.lead_ref), custom_call_target="tpu_custom_call" | custom-call | flops 6000000000 | bytes 3145728 | tf_op jit(solution)/shard_map/column_sums/pallas_call | solution.py:322
  41.9 5.2 %collective-permute-start.4 = (bf16[2,256,256]{2,1,0:T(8,128)(2,1)S(1)}, bf16[2,256,256]{2,1,0:T(8,128)(2,1)S(1)}, u32[]{:S(2)}, u32[]{:S(2)}) collective-permute-start(bf16[2,256,256]{2,1,0:T(8,128)(2,1)S(1)} %get-tuple-element.20.refs_2_), channel_id=1, source_target_pairs={{0,1},{2,3},{4,5},{6,7},{8,9},{10,11},{12,13},{14,15},{1,0},{3,2},... | collective-permute-start | bytes 786440 | tf_op jit(solution)/shard_map/ppermute | solution.py:421
  47.1 14.7 %collective-permute-start.6 = (bf16[2,256,256]{2,1,0:T(8,128)(2,1)S(1)}, bf16[2,256,256]{2,1,0:T(8,128)(2,1)S(1)}, u32[]{:S(2)}, u32[]{:S(2)}) collective-permute-start(bf16[2,256,256]{2,1,0:T(8,128)(2,1)S(1)} %get-tuple-element.20.refs_2_), channel_id=1, source_target_pairs={{1,2},{3,4},{5,6},{7,8},{9,10},{11,12},{13,14},{2,1},{4,3},{6,5},{... | collective-permute-start | bytes 786440 | tf_op jit(solution)/shard_map/ppermute | solution.py:421
  61.8 0.0 copy-done.1
  61.9 0.4 second_half.1.refs_2_
  62.3 1.9 %collective-permute-start = (bf16[2,256,256]{2,1,0:T(8,128)(2,1)S(1)}, bf16[2,256,256]{2,1,0:T(8,128)(2,1)S(1)}, u32[]{:S(2)}, u32[]{:S(2)}) collective-permute-start(bf16[2,256,256]{2,1,0:T(8,128)(2,1)S(1)} %second_half.1.refs_2_), channel_id=1, source_target_pairs={{0,1},{2,3},{4,5},{6,7},{8,9},{10,11},{12,13},{14,15},{1,0},{3,2},... | collective-permute-start | bytes 786440 | tf_op jit(solution)/shard_map/ppermute | solution.py:421
  64.2 3.9 %collective-permute-start.2 = (bf16[2,256,256]{2,1,0:T(8,128)(2,1)S(1)}, bf16[2,256,256]{2,1,0:T(8,128)(2,1)S(1)}, u32[]{:S(2)}, u32[]{:S(2)}) collective-permute-start(bf16[2,256,256]{2,1,0:T(8,128)(2,1)S(1)} %second_half.1.refs_2_), channel_id=1, source_target_pairs={{1,2},{3,4},{5,6},{7,8},{9,10},{11,12},{13,14},{2,1},{4,3},{6,5},{... | collective-permute-start | bytes 786440 | tf_op jit(solution)/shard_map/ppermute | solution.py:421
  68.2 0.0 collective-permute-done.4.refs_3_
  68.2 4.0 %collective-permute-start.5 = (bf16[2,256,256]{2,1,0:T(8,128)(2,1)S(1)}, bf16[2,256,256]{2,1,0:T(8,128)(2,1)S(1)}, u32[]{:S(2)}, u32[]{:S(2)}) collective-permute-start(bf16[2,256,256]{2,1,0:T(8,128)(2,1)S(1)} %collective-permute-done.4.refs_3_), channel_id=1, source_target_pairs={{1,2},{3,4},{5,6},{7,8},{9,10},{11,12},{13,14},{2,1},{4,3},{6,5},{... | collective-permute-start | bytes 786440 | tf_op jit(solution)/shard_map/ppermute | solution.py:421
  72.2 0.0 collective-permute-done.6.refs_1_
  72.2 1.9 %collective-permute-start.7 = (bf16[2,256,256]{2,1,0:T(8,128)(2,1)S(1)}, bf16[2,256,256]{2,1,0:T(8,128)(2,1)S(1)}, u32[]{:S(2)}, u32[]{:S(2)}) collective-permute-start(bf16[2,256,256]{2,1,0:T(8,128)(2,1)S(1)} %collective-permute-done.6.refs_1_), channel_id=1, source_target_pairs={{0,1},{2,3},{4,5},{6,7},{8,9},{10,11},{12,13},{14,15},{1,0},{3,2},... | collective-permute-start | bytes 786440 | tf_op jit(solution)/shard_map/ppermute | solution.py:421
  74.1 0.0 collective-permute-done.refs_3_
  74.2 3.9 %collective-permute-start.1 = (bf16[2,256,256]{2,1,0:T(8,128)(2,1)S(1)}, bf16[2,256,256]{2,1,0:T(8,128)(2,1)S(1)}, u32[]{:S(2)}, u32[]{:S(2)}) collective-permute-start(bf16[2,256,256]{2,1,0:T(8,128)(2,1)S(1)} %collective-permute-done.refs_3_), channel_id=1, source_target_pairs={{1,2},{3,4},{5,6},{7,8},{9,10},{11,12},{13,14},{2,1},{4,3},{6,5},{... | collective-permute-start | bytes 786440 | tf_op jit(solution)/shard_map/ppermute | solution.py:421
  78.1 0.0 collective-permute-done.2.refs_1_
  78.1 1.9 %collective-permute-start.3 = (bf16[2,256,256]{2,1,0:T(8,128)(2,1)S(1)}, bf16[2,256,256]{2,1,0:T(8,128)(2,1)S(1)}, u32[]{:S(2)}, u32[]{:S(2)}) collective-permute-start(bf16[2,256,256]{2,1,0:T(8,128)(2,1)S(1)} %collective-permute-done.2.refs_1_), channel_id=1, source_target_pairs={{0,1},{2,3},{4,5},{6,7},{8,9},{10,11},{12,13},{14,15},{1,0},{3,2},... | collective-permute-start | bytes 786440 | tf_op jit(solution)/shard_map/ppermute | solution.py:421
  80.0 3.0 %collective-permute-done.5.refs_0_ = bf16[2,256,256]{2,1,0:T(8,128)(2,1)S(1)} collective-permute-done((bf16[2,256,256]{2,1,0:T(8,128)(2,1)S(1)}, bf16[2,256,256]{2,1,0:T(8,128)(2,1)S(1)}, u32[]{:S(2)}, u32[]{:S(2)}) %collective-permute-start.5) | collective-permute-done | bytes 262176 | tf_op jit(solution)/shard_map/ppermute | solution.py:421
  83.0 0.0 collective-permute-done.7.refs_4_
  83.0 0.9 image.2.refs_8_
  83.9 4.4 %collective-permute-done.1.refs_0_ = bf16[2,256,256]{2,1,0:T(8,128)(2,1)S(1)} collective-permute-done((bf16[2,256,256]{2,1,0:T(8,128)(2,1)S(1)}, bf16[2,256,256]{2,1,0:T(8,128)(2,1)S(1)}, u32[]{:S(2)}, u32[]{:S(2)}) %collective-permute-start.1) | collective-permute-done | bytes 262176 | tf_op jit(solution)/shard_map/ppermute | solution.py:421
  88.4 0.0 collective-permute-done.3.refs_4_
  88.4 1.8 %image.3 = f32[2,512,256]{2,1,0:T(8,128)} custom-call(bf16[2,256,256]{2,1,0:T(8,128)(2,1)S(1)} %collective-permute-done.1.refs_0_, bf16[2,256,256]{2,1,0:T(8,128)(2,1)S(1)} %collective-permute-done.2.refs_1_, bf16[2,256,256]{2,1,0:T(8,128)(2,1)S(1)} %second_half.1.refs_2_, bf16[2,256,256]{2,1,0:T(8,128)(2,1)S(1)} %collective-permute-done.refs_3_, ...), custom_call_target="tpu_custom_call" | custom-call | flops 900000000 | bytes 4194304 | tf_op jit(solution)/shard_map/image/pallas_call | solution.py:406
Async XLA Ops:
  2.8 31.0 %all-to-all-start = ((bf16[64,16,256]{2,1,0:T(8,128)(2,1)}), bf16[64,16,256]{2,1,0:T(8,128)(2,1)S(1)}, u32[]{:S(2)}, u32[]{:S(2)}) async-start(bf16[64,16,256]{2,1,0:T(8,128)(2,1)} %bitcast.6), calls=%async_computation | async-start | bytes 1048576 | tf_op jit(solution)/shard_map/all_to_all | solution.py:436
  16.9 0.8 copy-start
  33.7 28.1 %copy-start.1 = (bf16[512,512]{1,0:T(8,128)(2,1)S(1)}, bf16[512,512]{1,0:T(8,128)(2,1)}, u32[]{:S(2)}) copy-start(bf16[512,512]{1,0:T(8,128)(2,1)} %copy-done) | copy-start | bytes 1572868
  41.9 26.2 %collective-permute-start.4 = (bf16[2,256,256]{2,1,0:T(8,128)(2,1)S(1)}, bf16[2,256,256]{2,1,0:T(8,128)(2,1)S(1)}, u32[]{:S(2)}, u32[]{:S(2)}) collective-permute-start(bf16[2,256,256]{2,1,0:T(8,128)(2,1)S(1)} %get-tuple-element.20.refs_2_), channel_id=1, source_target_pairs={{0,1},{2,3},{4,5},{6,7},{8,9},{10,11},{12,13},{14,15},{1,0},{3,2},... | collective-permute-start | bytes 786440 | tf_op jit(solution)/shard_map/ppermute | solution.py:421
  47.1 25.1 %collective-permute-start.6 = (bf16[2,256,256]{2,1,0:T(8,128)(2,1)S(1)}, bf16[2,256,256]{2,1,0:T(8,128)(2,1)S(1)}, u32[]{:S(2)}, u32[]{:S(2)}) collective-permute-start(bf16[2,256,256]{2,1,0:T(8,128)(2,1)S(1)} %get-tuple-element.20.refs_2_), channel_id=1, source_target_pairs={{1,2},{3,4},{5,6},{7,8},{9,10},{11,12},{13,14},{2,1},{4,3},{6,5},{... | collective-permute-start | bytes 786440 | tf_op jit(solution)/shard_map/ppermute | solution.py:421
  62.3 11.8 %collective-permute-start = (bf16[2,256,256]{2,1,0:T(8,128)(2,1)S(1)}, bf16[2,256,256]{2,1,0:T(8,128)(2,1)S(1)}, u32[]{:S(2)}, u32[]{:S(2)}) collective-permute-start(bf16[2,256,256]{2,1,0:T(8,128)(2,1)S(1)} %second_half.1.refs_2_), channel_id=1, source_target_pairs={{0,1},{2,3},{4,5},{6,7},{8,9},{10,11},{12,13},{14,15},{1,0},{3,2},... | collective-permute-start | bytes 786440 | tf_op jit(solution)/shard_map/ppermute | solution.py:421
  64.2 13.9 %collective-permute-start.2 = (bf16[2,256,256]{2,1,0:T(8,128)(2,1)S(1)}, bf16[2,256,256]{2,1,0:T(8,128)(2,1)S(1)}, u32[]{:S(2)}, u32[]{:S(2)}) collective-permute-start(bf16[2,256,256]{2,1,0:T(8,128)(2,1)S(1)} %second_half.1.refs_2_), channel_id=1, source_target_pairs={{1,2},{3,4},{5,6},{7,8},{9,10},{11,12},{13,14},{2,1},{4,3},{6,5},{... | collective-permute-start | bytes 786440 | tf_op jit(solution)/shard_map/ppermute | solution.py:421
  68.2 14.9 %collective-permute-start.5 = (bf16[2,256,256]{2,1,0:T(8,128)(2,1)S(1)}, bf16[2,256,256]{2,1,0:T(8,128)(2,1)S(1)}, u32[]{:S(2)}, u32[]{:S(2)}) collective-permute-start(bf16[2,256,256]{2,1,0:T(8,128)(2,1)S(1)} %collective-permute-done.4.refs_3_), channel_id=1, source_target_pairs={{1,2},{3,4},{5,6},{7,8},{9,10},{11,12},{13,14},{2,1},{4,3},{6,5},{... | collective-permute-start | bytes 786440 | tf_op jit(solution)/shard_map/ppermute | solution.py:421
  72.2 10.8 %collective-permute-start.7 = (bf16[2,256,256]{2,1,0:T(8,128)(2,1)S(1)}, bf16[2,256,256]{2,1,0:T(8,128)(2,1)S(1)}, u32[]{:S(2)}, u32[]{:S(2)}) collective-permute-start(bf16[2,256,256]{2,1,0:T(8,128)(2,1)S(1)} %collective-permute-done.6.refs_1_), channel_id=1, source_target_pairs={{0,1},{2,3},{4,5},{6,7},{8,9},{10,11},{12,13},{14,15},{1,0},{3,2},... | collective-permute-start | bytes 786440 | tf_op jit(solution)/shard_map/ppermute | solution.py:421
  74.2 14.2 %collective-permute-start.1 = (bf16[2,256,256]{2,1,0:T(8,128)(2,1)S(1)}, bf16[2,256,256]{2,1,0:T(8,128)(2,1)S(1)}, u32[]{:S(2)}, u32[]{:S(2)}) collective-permute-start(bf16[2,256,256]{2,1,0:T(8,128)(2,1)S(1)} %collective-permute-done.refs_3_), channel_id=1, source_target_pairs={{1,2},{3,4},{5,6},{7,8},{9,10},{11,12},{13,14},{2,1},{4,3},{6,5},{... | collective-permute-start | bytes 786440 | tf_op jit(solution)/shard_map/ppermute | solution.py:421
  78.1 10.3 %collective-permute-start.3 = (bf16[2,256,256]{2,1,0:T(8,128)(2,1)S(1)}, bf16[2,256,256]{2,1,0:T(8,128)(2,1)S(1)}, u32[]{:S(2)}, u32[]{:S(2)}) collective-permute-start(bf16[2,256,256]{2,1,0:T(8,128)(2,1)S(1)} %collective-permute-done.2.refs_1_), channel_id=1, source_target_pairs={{0,1},{2,3},{4,5},{6,7},{8,9},{10,11},{12,13},{14,15},{1,0},{3,2},... | collective-permute-start | bytes 786440 | tf_op jit(solution)/shard_map/ppermute | solution.py:421

commit v3 on v2

--- a/solution.py
+++ b/solution.py
@@ -15,10 +15,11 @@
 REACH = 2
 OFFSETS = 2 * REACH + 1
 CAP = 3
-SLOTS = OFFSETS * CAP
+SLOTS = (OFFSETS + 1) * CAP
 HALF = TH // 2
 PARTS = 4
-ROWS = 16
+ROWS = 24
+WORDS = 14
 SPREAD = 16.0
 SCALE = 1.0 / math.sqrt(TH * TW)
 
@@ -116,6 +117,10 @@
     )()
 
 
+def over(value, divisor):
+    return (value * (65536 // divisor + 1)) >> 16
+
+
 def pack_kernel(amp_at, tilt_at, owner_at, row_at, col_at, out_at, *scratch):
     amp_ref, tilt_ref, owner_ref, row_ref, col_ref, out_ref, sems, out_sems = scratch
     copies = [
@@ -136,12 +141,16 @@
     total = out_ref.shape[0]
     sub, lane = iota((count, count), 0), iota((count, count), 1)
     at = iota((total, count), 0)
-    wanted = CAP * (at >> 4) + (at & 15) - CAP * REACH
-    wanted = jnp.where((at & 15) == SLOTS, -1, wanted).astype(F32)
+    chip = over(at, ROWS)
+    slot = at - ROWS * chip
+    wanted = 2 * CAP * chip + slot - CAP * REACH
+    wanted = jnp.where(slot >= SLOTS, -1, wanted).astype(F32)
     old = iota((256, 256), 0)
-    new = ((old >> 4) & 3) * 64 + (old >> 6) * 16 + (old & 15)
+    new = ((old >> 4) & 7) * 32 + (old >> 7) * 16 + (old & 15)
     order = jnp.where(iota((256, 256), 1) == new, 1.0, 0.0).astype(BF16)
-    repeat = jnp.where((iota((16, 256), 1) & 15) == iota((16, 256), 0), 1.0, 0.0).astype(BF16)
+    word = iota((16, 256), 1)
+    word = word - WORDS * over(word, WORDS)
+    repeat = jnp.where(word == iota((16, 256), 0), 1.0, 0.0).astype(BF16)
     for copy in copies:
         copy.wait()
     row, col = row_ref[...], col_ref[...]
@@ -182,7 +191,8 @@
     ).astype(BF16)
     both = jnp.concatenate([amp, extras], axis=1)
     part = total // PARTS
-    keep = (iota((part, 256), 1) >> 4) == (iota((part, 256), 0) & 15)
+    line = iota((part, 256), 0)
+    keep = over(iota((part, 256), 1), WORDS) == line - ROWS * over(line, ROWS)
     last = iota((part // ROWS, ROWS, 256), 1) == SLOTS
     sends = []
     for k in range(PARTS):
@@ -199,11 +209,11 @@
         send.wait()
 
 
-def pack(amplitude, tilt, owner, row_offset, col_offset, wide_count):
+def pack(amplitude, tilt, owner, row_offset, col_offset, chip_count):
     count = amplitude.shape[0]
     return pl.pallas_call(
         pack_kernel,
-        out_shape=jax.ShapeDtypeStruct((wide_count * ROWS, 256), BF16),
+        out_shape=jax.ShapeDtypeStruct((chip_count * ROWS, 256), BF16),
         in_specs=[pl.BlockSpec(memory_space=pl.ANY)] * 5,
         out_specs=pl.BlockSpec(memory_space=pl.ANY),
         scratch_shapes=[
@@ -212,7 +222,7 @@
             pltpu.VMEM((1, count), jnp.int32),
             pltpu.VMEM((1, count), jnp.int32),
             pltpu.VMEM((1, count), jnp.int32),
-            pltpu.VMEM((wide_count * ROWS, 256), BF16),
+            pltpu.VMEM((chip_count * ROWS, 256), BF16),
             pltpu.SemaphoreType.DMA((5,)),
             pltpu.SemaphoreType.DMA((PARTS,)),
         ],
@@ -245,33 +255,34 @@
     out_ref[1] = ((product[:TW, HALF:] + product[TW:, :HALF]) * SCALE).astype(BF16)
 
 
-def column_kernel(inc_ref, lead_ref, out_ref, value_ref, facets_lo, facets_hi, param, plane, total):
-    fblk_ref, grow_ref = lead_ref.at[:TH], lead_ref.at[TH:]
-    sources = inc_ref.shape[0] // ROWS
-    lanes = 4 * sources
-    facets_lo[...] = inc_ref[:, :128].astype(F32)
-    facets_hi[...] = inc_ref[:, 128:].astype(F32)
-    total[...] = jnp.zeros_like(total)
-    pick = pl.ds(SLOTS, sources, stride=ROWS)
-    extras = jnp.concatenate([facets_lo[pick, :], facets_hi[pick, :]], axis=1)
-    entry = iota(extras.shape, 1) & 15
-    tilt = extras + pltpu.roll(extras, 253, 1) + pltpu.roll(extras, 250, 1)
-    tilt = jnp.where(entry < 3, tilt, pltpu.roll(tilt, 3, 1))
-    turn_r, turn_i = cis(tilt)
-    param[...] = jnp.where(entry < 3, turn_r, jnp.where(entry < 6, turn_i, extras))
-    mx = iota((2 * TW, 1), 0) & (TW - 1)
-    member = iota((8, lanes), 1) // sources
-    residue = 4 * iota((8, lanes), 0) + member
-    spot = iota((128, lanes), 0).astype(F32)
-    aside = iota((sources, 128), 1) < 64
-
-    def one_slot(i):
-        pick = pl.ds(i, sources, stride=ROWS)
-        low, high = facets_lo[pick, :], facets_hi[pick, :]
-        mine = pltpu.roll(param[...], (320 - 16 * i) & 255, 1)[:, :128]
-        blocks = [low, pltpu.roll(low, 64, 1), high, pltpu.roll(high, 64, 1)]
+class Arrivals:
+    def __init__(self, inc_ref, facets_lo, facets_hi, param):
+        self.sources = inc_ref.shape[0] // ROWS
+        self.refs = facets_lo, facets_hi, param
+        facets_lo[...] = inc_ref[:, :128].astype(F32)
+        facets_hi[...] = inc_ref[:, 128:].astype(F32)
+        pick = pl.ds(SLOTS, self.sources, stride=ROWS)
+        extras = jnp.concatenate([facets_lo[pick, :], facets_hi[pick, :]], axis=1)
+        entry = iota(extras.shape, 1)
+        entry = entry - WORDS * over(entry, WORDS)
+        tilt = extras + pltpu.roll(extras, 253, 1) + pltpu.roll(extras, 250, 1)
+        tilt = jnp.where(entry < 3, tilt, pltpu.roll(tilt, 3, 1))
+        turn_r, turn_i = cis(tilt)
+        param[...] = jnp.where(entry < 3, turn_r, jnp.where(entry < 6, turn_i, extras))
+
+    def slot(self, i):
+        facets_lo, facets_hi, param = self.refs
+        lanes = 8 * self.sources
+        member = iota((8, lanes), 1) // self.sources
+        residue = 8 * iota((8, lanes), 0) + member
+        aside = iota((self.sources, 128), 1) < 32
+        pick = pl.ds(i, self.sources, stride=ROWS)
+        mine = pltpu.roll(param[...], (288 - WORDS * i) & 255, 1)[:, :128]
+        blocks = []
+        for half in (facets_lo[pick, :], facets_hi[pick, :]):
+            blocks += [half] + [pltpu.roll(half, 128 - 32 * m, 1) for m in (1, 2, 3)]
         turned = jnp.concatenate([jnp.where(aside, block, mine) for block in blocks], axis=0).T
-        par = turned[64:80]
+        par = turned[32:48]
         block, turn_u, col = [par[k : k + 1].astype(jnp.int32) for k in (9, 10, 11)]
         row_r, row_i = power_of(
             par[0:1], par[3:4], (residue - turn_u) & 15, par[2:3], par[5:6]
@@ -285,9 +296,17 @@
         window = jnp.where((ahead & -16) == 0, 1.0, 0.0).astype(BF16)
         return turned, row_r, row_i, col_r, col_i, spots, window
 
-    def one_column(j, carry):
-        slots = [one_slot(CAP * j + k) for k in range(CAP)]
-        for group in range(4):
+
+def column_kernel(mine_ref, beside_ref, lead_ref, out_ref, value_ref, *scratch):
+    plane, total = scratch[-2:]
+    arrivals = [Arrivals(mine_ref, *scratch[0:3]), Arrivals(beside_ref, *scratch[3:6])]
+    fblk_ref, grow_ref = lead_ref.at[:TH], lead_ref.at[TH:]
+    core = lax.axis_index("wide") & 1
+    mx = iota((2 * TW, 1), 0) & (TW - 1)
+    spot = iota((256, 8 * arrivals[0].sources), 0).astype(F32)
+    for j in range(OFFSETS):
+        slots = [part.slot(CAP * (core + j) + k) for part in arrivals for k in range(CAP)]
+        for group in range(2):
             spreads, hots = [], []
             for turned, row_r, row_i, col_r, col_i, spots, window in slots:
                 patch = turned[16 * group : 16 * group + 16]
@@ -306,38 +325,36 @@
                 )
             spread = jnp.concatenate(spreads, axis=1)
             hot = jnp.concatenate(hots, axis=1)
-            plane[:, 128 * group : 128 * group + 128] = mm(spread, hot, NT).astype(BF16)
+            plane[j % 2, :, 256 * group : 256 * group + 256] = mm(spread, hot, NT).astype(BF16)
         weight = reach_weight(mx, TW, float(REACH - j))
-        total[...] += weight * mm(fblk_ref[...], plane[...])
-        return carry
-
-    for j in range(OFFSETS):
-        one_column(j, 0)
+        term = weight * mm(fblk_ref[...], plane[j % 2])
+        total[...] = term if j == 0 else total[...] + term
     value = total[...].astype(BF16)
     value_ref[...] = value
     row_transform(value, grow_ref, out_ref)
 
 
-def column_sums(incoming, lead):
+def column_sums(mine, beside, lead):
+    facets = [
+        pltpu.VMEM((mine.shape[0], 128), F32),
+        pltpu.VMEM((mine.shape[0], 128), F32),
+        pltpu.VMEM((mine.shape[0] // ROWS, 256), F32),
+    ]
     return pl.pallas_call(
         column_kernel,
         out_shape=(
             jax.ShapeDtypeStruct((2, TW, HALF), BF16),
             jax.ShapeDtypeStruct((2 * TW, TH), BF16),
         ),
-        in_specs=[pl.BlockSpec(memory_space=pltpu.VMEM)] * 2,
+        in_specs=[pl.BlockSpec(memory_space=pltpu.VMEM)] * 3,
         out_specs=tuple([pl.BlockSpec(memory_space=pltpu.VMEM)] * 2),
-        scratch_shapes=[
-            pltpu.VMEM((incoming.shape[0], 128), F32),
-            pltpu.VMEM((incoming.shape[0], 128), F32),
-            pltpu.VMEM((incoming.shape[0] // ROWS, 256), F32),
-            pltpu.VMEM((2 * TW, TH), BF16),
-            pltpu.VMEM((2 * TW, TH), F32),
-        ],
-        compiler_params=pltpu.CompilerParams(vmem_limit_bytes=20 << 20),
-        cost_estimate=pl.CostEstimate(flops=6_000_000_000, bytes_accessed=3 << 20, transcendentals=40_000),
+        scratch_shapes=facets
+        + facets
+        + [pltpu.VMEM((2, 2 * TW, TH), BF16), pltpu.VMEM((2 * TW, TH), F32)],
+        compiler_params=pltpu.CompilerParams(vmem_limit_bytes=24 << 20),
+        cost_estimate=pl.CostEstimate(flops=8_000_000_000, bytes_accessed=3 << 20, transcendentals=40_000),
         name="column_sums",
-    )(incoming, lead)
+    )(mine, beside, lead)
 
 
 def second_kernel(value_ref, grow_ref, out_ref):
@@ -431,12 +448,19 @@
 
 def local(amplitude, tilt, owner, row_offset, col_offset):
     wide_count = lax.axis_size("wide")
+    chip_count = wide_count // 2
     lead, grow_b, hblk, kr_a, ki_a, kr_b, ki_b = make_tables()
-    outgoing = pack(amplitude, tilt, owner, row_offset, col_offset, wide_count)
-    incoming = lax.all_to_all(
-        outgoing.reshape(wide_count, ROWS, 256), "wide", split_axis=0, concat_axis=0, tiled=True
-    ).reshape(wide_count * ROWS, 256)
-    first, value = column_sums(incoming, lead)
+    outgoing = pack(amplitude, tilt, owner, row_offset, col_offset, chip_count)
+    mine = lax.all_to_all(
+        outgoing.reshape(chip_count, ROWS, 256),
+        "wide",
+        split_axis=0,
+        concat_axis=0,
+        tiled=True,
+        axis_index_groups=[list(range(core, wide_count, 2)) for core in range(2)],
+    ).reshape(chip_count * ROWS, 256)
+    beside = lax.ppermute(mine, "wide", [(at, at ^ 1) for at in range(wide_count)])
+    first, value = column_sums(mine, beside, lead)
     second = second_half(value, grow_b)
     partial = image_of(0, narrow_pieces(first), (hblk, kr_a, ki_a), ())
     return image_of(1, narrow_pieces(second), (hblk, kr_b, ki_b), (partial,))

time: 90.6 us -> 91.9 us (1.014)
  the two profiles are of different devices: /device:TPU:22 before, /device:TPU:18 now
where the time goes in v3:
time: 91.9 us; the launch traced here: 91.4 us
  starting transfers between devices  39.5 us (43%)
  blocking collectives  29.6 us (32%)
  Pallas kernels  15.2 us (17%)
  waiting for transfers between devices  7.01 us (8%)
    ppermute x8, starting transfers between devices, swap(): lax.ppermute(value, 'narrow', pairs + [(high, low) for low, high in pairs])  37.6 us
    all_to_all x1, blocking collectives, local(): lax.all_to_all(outgoing.reshape(chip_count, ROWS, 256), 'wide', split_axi...  29.6 us
    pallas_call x1, Pallas kernels, column_sums(): pl.pallas_call(column_kernel, out_shape=(jax.ShapeDtypeStruct((2, TW, HAL...  7.9 us
    ppermute x8, waiting for transfers between devices, swap(): lax.ppermute(value, 'narrow', pairs + [(high, low) for low, high in pairs])  6.81 us
    pallas_call x1, Pallas kernels, pack(): pl.pallas_call(pack_kernel, out_shape=jax.ShapeDtypeStruct((chip_count *...  2.69 us
    pallas_call x2, Pallas kernels, image_of(): pl.pallas_call(functools.partial(image_kernel, half), out_shape=jax.Shape...  2.68 us
    ppermute x1, starting transfers between devices, local(): lax.ppermute(mine, 'wide', [(at, at ^ 1) for at in range(wide_count)])  1.91 us
  transfers between devices with their start and end apart: 9, of which 3 were waited for; matrix products, arithmetic and copies ran while one was open for 0% of the time, Pallas kernels for 3%

profile of v3, /device:TPU:18, one launch (start us, length us, event | category | flops | bytes accessed | tf_op | source)
XLA Modules:
  0.0 91.4 jit_solution(1134010579386290747)
XLA Ops:
  0.0 2.7 %pack.1 = bf16[768,256]{1,0:T(8,128)(2,1)} custom-call(f32[64,256]{1,0:T(8,128)} %amp_at.1, f32[3,64]{1,0:T(4,128)} %tilt_at.1, s32[1,64]{1,0:T(1,128)} %bitcast.8, s32[1,64]{1,0:T(1,128)} %bitcast.9, s32[1,64]{1,0:T(1,128)} %bitcast.10), custom_call_target="tpu_custom_call" | custom-call | tf_op jit(solution)/shard_map/pack/pallas_call | solution.py:214
  2.7 29.6 %all_to_all.5 = bf16[32,24,256]{2,1,0:T(8,128)(2,1)S(1)} all-to-all(bf16[32,24,256]{2,1,0:T(8,128)(2,1)} %bitcast.7), channel_id=1, replica_groups={{0,32,64,96,128,160,192,224,256,288,320,352,384,416,448,480,512,544,576..., dimensions={0} | all-to-all | bytes 786432 | tf_op jit(solution)/shard_map/all_to_all | solution.py:454
  32.3 1.9 %collective-permute-start = (bf16[768,256]{1,0:T(8,128)(2,1)S(1)}, bf16[768,256]{1,0:T(8,128)(2,1)S(1)}, u32[]{:S(2)}, u32[]{:S(2)}) collective-permute-start(bf16[768,256]{1,0:T(8,128)(2,1)S(1)} %bitcast.5), channel_id=1, source_target_pairs={{0,16},{16,0},{32,48},{48,32},{64,80},{80,64},{96,112},{112,96},{1... | collective-permute-start | bytes 1179656 | tf_op jit(solution)/shard_map/ppermute | solution.py:462
  34.2 1.5 %tables.1 = (bf16[1024,512]{1,0:T(8,128)(2,1)S(1)}, bf16[512,512]{1,0:T(8,128)(2,1)S(1)}, bf16[512,512]{1,0:T(8,128)(2,1)S(1)}, bf16[512,256]{1,0:T(8,128)(2,1)S...) custom-call(), custom_call_target="tpu_custom_call" | custom-call | flops 8000000 | bytes 3145728 | tf_op jit(solution)/shard_map/tables/pallas_call | solution.py:110
  35.7 0.2 collective-permute-done.beside_ref
  35.9 7.9 %column_sums.1 = (bf16[2,256,256]{2,1,0:T(8,128)(2,1)S(1)}, bf16[512,512]{1,0:T(8,128)(2,1)S(1)}) custom-call(bf16[768,256]{1,0:T(8,128)(2,1)S(1)} %bitcast.6, bf16[768,256]{1,0:T(8,128)(2,1)S(1)} %collective-permute-done.beside_ref, bf16[1024,512]{1,0:T(8,128)(2,1)S(1)} %get-tuple-element.14.lead_ref), custom_call_target="tpu_custom_call" | custom-call | flops 8000000000 | bytes 3145728 | tf_op jit(solution)/shard_map/column_sums/pallas_call | solution.py:343
  43.8 5.2 %collective-permute-start.5 = (bf16[2,256,256]{2,1,0:T(8,128)(2,1)S(1)}, bf16[2,256,256]{2,1,0:T(8,128)(2,1)S(1)}, u32[]{:S(2)}, u32[]{:S(2)}) collective-permute-start(bf16[2,256,256]{2,1,0:T(8,128)(2,1)S(1)} %get-tuple-element.20.refs_2_), channel_id=1, source_target_pairs={{0,1},{2,3},{4,5},{6,7},{8,9},{10,11},{12,13},{14,15},{1,0},{3,2},... | collective-permute-start | bytes 786440 | tf_op jit(solution)/shard_map/ppermute | solution.py:438
  49.1 14.7 %collective-permute-start.7 = (bf16[2,256,256]{2,1,0:T(8,128)(2,1)S(1)}, bf16[2,256,256]{2,1,0:T(8,128)(2,1)S(1)}, u32[]{:S(2)}, u32[]{:S(2)}) collective-permute-start(bf16[2,256,256]{2,1,0:T(8,128)(2,1)S(1)} %get-tuple-element.20.refs_2_), channel_id=1, source_target_pairs={{1,2},{3,4},{5,6},{7,8},{9,10},{11,12},{13,14},{2,1},{4,3},{6,5},{... | collective-permute-start | bytes 786440 | tf_op jit(solution)/shard_map/ppermute | solution.py:438
  63.8 0.4 second_half.1.refs_2_
  64.2 1.9 %collective-permute-start.1 = (bf16[2,256,256]{2,1,0:T(8,128)(2,1)S(1)}, bf16[2,256,256]{2,1,0:T(8,128)(2,1)S(1)}, u32[]{:S(2)}, u32[]{:S(2)}) collective-permute-start(bf16[2,256,256]{2,1,0:T(8,128)(2,1)S(1)} %second_half.1.refs_2_), channel_id=1, source_target_pairs={{0,1},{2,3},{4,5},{6,7},{8,9},{10,11},{12,13},{14,15},{1,0},{3,2},... | collective-permute-start | bytes 786440 | tf_op jit(solution)/shard_map/ppermute | solution.py:438
  66.1 3.9 %collective-permute-start.3 = (bf16[2,256,256]{2,1,0:T(8,128)(2,1)S(1)}, bf16[2,256,256]{2,1,0:T(8,128)(2,1)S(1)}, u32[]{:S(2)}, u32[]{:S(2)}) collective-permute-start(bf16[2,256,256]{2,1,0:T(8,128)(2,1)S(1)} %second_half.1.refs_2_), channel_id=1, source_target_pairs={{1,2},{3,4},{5,6},{7,8},{9,10},{11,12},{13,14},{2,1},{4,3},{6,5},{... | collective-permute-start | bytes 786440 | tf_op jit(solution)/shard_map/ppermute | solution.py:438
  70.1 0.0 collective-permute-done.5.refs_3_
  70.1 4.0 %collective-permute-start.6 = (bf16[2,256,256]{2,1,0:T(8,128)(2,1)S(1)}, bf16[2,256,256]{2,1,0:T(8,128)(2,1)S(1)}, u32[]{:S(2)}, u32[]{:S(2)}) collective-permute-start(bf16[2,256,256]{2,1,0:T(8,128)(2,1)S(1)} %collective-permute-done.5.refs_3_), channel_id=1, source_target_pairs={{1,2},{3,4},{5,6},{7,8},{9,10},{11,12},{13,14},{2,1},{4,3},{6,5},{... | collective-permute-start | bytes 786440 | tf_op jit(solution)/shard_map/ppermute | solution.py:438
  74.1 0.0 collective-permute-done.7.refs_1_
  74.1 1.9 %collective-permute-start.8 = (bf16[2,256,256]{2,1,0:T(8,128)(2,1)S(1)}, bf16[2,256,256]{2,1,0:T(8,128)(2,1)S(1)}, u32[]{:S(2)}, u32[]{:S(2)}) collective-permute-start(bf16[2,256,256]{2,1,0:T(8,128)(2,1)S(1)} %collective-permute-done.7.refs_1_), channel_id=1, source_target_pairs={{0,1},{2,3},{4,5},{6,7},{8,9},{10,11},{12,13},{14,15},{1,0},{3,2},... | collective-permute-start | bytes 786440 | tf_op jit(solution)/shard_map/ppermute | solution.py:438
  76.1 0.0 collective-permute-done.1.refs_3_
  76.1 3.9 %collective-permute-start.2 = (bf16[2,256,256]{2,1,0:T(8,128)(2,1)S(1)}, bf16[2,256,256]{2,1,0:T(8,128)(2,1)S(1)}, u32[]{:S(2)}, u32[]{:S(2)}) collective-permute-start(bf16[2,256,256]{2,1,0:T(8,128)(2,1)S(1)} %collective-permute-done.1.refs_3_), channel_id=1, source_target_pairs={{1,2},{3,4},{5,6},{7,8},{9,10},{11,12},{13,14},{2,1},{4,3},{6,5},{... | collective-permute-start | bytes 786440 | tf_op jit(solution)/shard_map/ppermute | solution.py:438
  80.0 0.0 collective-permute-done.3.refs_1_
  80.0 1.9 %collective-permute-start.4 = (bf16[2,256,256]{2,1,0:T(8,128)(2,1)S(1)}, bf16[2,256,256]{2,1,0:T(8,128)(2,1)S(1)}, u32[]{:S(2)}, u32[]{:S(2)}) collective-permute-start(bf16[2,256,256]{2,1,0:T(8,128)(2,1)S(1)} %collective-permute-done.3.refs_1_), channel_id=1, source_target_pairs={{0,1},{2,3},{4,5},{6,7},{8,9},{10,11},{12,13},{14,15},{1,0},{3,2},... | collective-permute-start | bytes 786440 | tf_op jit(solution)/shard_map/ppermute | solution.py:438
  81.9 3.0 %collective-permute-done.6.refs_0_ = bf16[2,256,256]{2,1,0:T(8,128)(2,1)S(1)} collective-permute-done((bf16[2,256,256]{2,1,0:T(8,128)(2,1)S(1)}, bf16[2,256,256]{2,1,0:T(8,128)(2,1)S(1)}, u32[]{:S(2)}, u32[]{:S(2)}) %collective-permute-start.6) | collective-permute-done | bytes 262176 | tf_op jit(solution)/shard_map/ppermute | solution.py:438
  84.9 0.0 collective-permute-done.8.refs_4_
  84.9 0.9 image.2.refs_8_
  85.8 3.8 %collective-permute-done.2.refs_0_ = bf16[2,256,256]{2,1,0:T(8,128)(2,1)S(1)} collective-permute-done((bf16[2,256,256]{2,1,0:T(8,128)(2,1)S(1)}, bf16[2,256,256]{2,1,0:T(8,128)(2,1)S(1)}, u32[]{:S(2)}, u32[]{:S(2)}) %collective-permute-start.2) | collective-permute-done | bytes 262176 | tf_op jit(solution)/shard_map/ppermute | solution.py:438
  89.6 0.0 collective-permute-done.4.refs_4_
  89.6 1.8 %image.3 = f32[2,512,256]{2,1,0:T(8,128)} custom-call(bf16[2,256,256]{2,1,0:T(8,128)(2,1)S(1)} %collective-permute-done.2.refs_0_, bf16[2,256,256]{2,1,0:T(8,128)(2,1)S(1)} %collective-permute-done.3.refs_1_, bf16[2,256,256]{2,1,0:T(8,128)(2,1)S(1)} %second_half.1.refs_2_, bf16[2,256,256]{2,1,0:T(8,128)(2,1)S(1)} %collective-permute-done.1.refs_3_, ...), custom_call_target="tpu_custom_call" | custom-call | flops 900000000 | bytes 4194304 | tf_op jit(solution)/shard_map/image/pallas_call | solution.py:423
Async XLA Ops:
  32.3 3.6 %collective-permute-start = (bf16[768,256]{1,0:T(8,128)(2,1)S(1)}, bf16[768,256]{1,0:T(8,128)(2,1)S(1)}, u32[]{:S(2)}, u32[]{:S(2)}) collective-permute-start(bf16[768,256]{1,0:T(8,128)(2,1)S(1)} %bitcast.5), channel_id=1, source_target_pairs={{0,16},{16,0},{32,48},{48,32},{64,80},{80,64},{96,112},{112,96},{1... | collective-permute-start | bytes 1179656 | tf_op jit(solution)/shard_map/ppermute | solution.py:462
  43.8 26.3 %collective-permute-start.5 = (bf16[2,256,256]{2,1,0:T(8,128)(2,1)S(1)}, bf16[2,256,256]{2,1,0:T(8,128)(2,1)S(1)}, u32[]{:S(2)}, u32[]{:S(2)}) collective-permute-start(bf16[2,256,256]{2,1,0:T(8,128)(2,1)S(1)} %get-tuple-element.20.refs_2_), channel_id=1, source_target_pairs={{0,1},{2,3},{4,5},{6,7},{8,9},{10,11},{12,13},{14,15},{1,0},{3,2},... | collective-permute-start | bytes 786440 | tf_op jit(solution)/shard_map/ppermute | solution.py:438
  49.1 25.0 %collective-permute-start.7 = (bf16[2,256,256]{2,1,0:T(8,128)(2,1)S(1)}, bf16[2,256,256]{2,1,0:T(8,128)(2,1)S(1)}, u32[]{:S(2)}, u32[]{:S(2)}) collective-permute-start(bf16[2,256,256]{2,1,0:T(8,128)(2,1)S(1)} %get-tuple-element.20.refs_2_), channel_id=1, source_target_pairs={{1,2},{3,4},{5,6},{7,8},{9,10},{11,12},{13,14},{2,1},{4,3},{6,5},{... | collective-permute-start | bytes 786440 | tf_op jit(solution)/shard_map/ppermute | solution.py:438
  64.2 11.8 %collective-permute-start.1 = (bf16[2,256,256]{2,1,0:T(8,128)(2,1)S(1)}, bf16[2,256,256]{2,1,0:T(8,128)(2,1)S(1)}, u32[]{:S(2)}, u32[]{:S(2)}) collective-permute-start(bf16[2,256,256]{2,1,0:T(8,128)(2,1)S(1)} %second_half.1.refs_2_), channel_id=1, source_target_pairs={{0,1},{2,3},{4,5},{6,7},{8,9},{10,11},{12,13},{14,15},{1,0},{3,2},... | collective-permute-start | bytes 786440 | tf_op jit(solution)/shard_map/ppermute | solution.py:438
  66.1 13.9 %collective-permute-start.3 = (bf16[2,256,256]{2,1,0:T(8,128)(2,1)S(1)}, bf16[2,256,256]{2,1,0:T(8,128)(2,1)S(1)}, u32[]{:S(2)}, u32[]{:S(2)}) collective-permute-start(bf16[2,256,256]{2,1,0:T(8,128)(2,1)S(1)} %second_half.1.refs_2_), channel_id=1, source_target_pairs={{1,2},{3,4},{5,6},{7,8},{9,10},{11,12},{13,14},{2,1},{4,3},{6,5},{... | collective-permute-start | bytes 786440 | tf_op jit(solution)/shard_map/ppermute | solution.py:438
  70.1 14.8 %collective-permute-start.6 = (bf16[2,256,256]{2,1,0:T(8,128)(2,1)S(1)}, bf16[2,256,256]{2,1,0:T(8,128)(2,1)S(1)}, u32[]{:S(2)}, u32[]{:S(2)}) collective-permute-start(bf16[2,256,256]{2,1,0:T(8,128)(2,1)S(1)} %collective-permute-done.5.refs_3_), channel_id=1, source_target_pairs={{1,2},{3,4},{5,6},{7,8},{9,10},{11,12},{13,14},{2,1},{4,3},{6,5},{... | collective-permute-start | bytes 786440 | tf_op jit(solution)/shard_map/ppermute | solution.py:438
  74.1 10.8 %collective-permute-start.8 = (bf16[2,256,256]{2,1,0:T(8,128)(2,1)S(1)}, bf16[2,256,256]{2,1,0:T(8,128)(2,1)S(1)}, u32[]{:S(2)}, u32[]{:S(2)}) collective-permute-start(bf16[2,256,256]{2,1,0:T(8,128)(2,1)S(1)} %collective-permute-done.7.refs_1_), channel_id=1, source_target_pairs={{0,1},{2,3},{4,5},{6,7},{8,9},{10,11},{12,13},{14,15},{1,0},{3,2},... | collective-permute-start | bytes 786440 | tf_op jit(solution)/shard_map/ppermute | solution.py:438
  76.1 13.6 %collective-permute-start.2 = (bf16[2,256,256]{2,1,0:T(8,128)(2,1)S(1)}, bf16[2,256,256]{2,1,0:T(8,128)(2,1)S(1)}, u32[]{:S(2)}, u32[]{:S(2)}) collective-permute-start(bf16[2,256,256]{2,1,0:T(8,128)(2,1)S(1)} %collective-permute-done.1.refs_3_), channel_id=1, source_target_pairs={{1,2},{3,4},{5,6},{7,8},{9,10},{11,12},{13,14},{2,1},{4,3},{6,5},{... | collective-permute-start | bytes 786440 | tf_op jit(solution)/shard_map/ppermute | solution.py:438
  80.0 9.6 %collective-permute-start.4 = (bf16[2,256,256]{2,1,0:T(8,128)(2,1)S(1)}, bf16[2,256,256]{2,1,0:T(8,128)(2,1)S(1)}, u32[]{:S(2)}, u32[]{:S(2)}) collective-permute-start(bf16[2,256,256]{2,1,0:T(8,128)(2,1)S(1)} %collective-permute-done.3.refs_1_), channel_id=1, source_target_pairs={{0,1},{2,3},{4,5},{6,7},{8,9},{10,11},{12,13},{14,15},{1,0},{3,2},... | collective-permute-start | bytes 786440 | tf_op jit(solution)/shard_map/ppermute | solution.py:438

commit v4 on v2

--- a/solution.py
+++ b/solution.py
@@ -361,7 +361,7 @@
     pieces = refs[:OFFSETS]
     hblk_ref, kr_ref, ki_ref = refs[OFFSETS : OFFSETS + 3]
     my = iota((1, HALF), 1) + HALF * half
-    weights = [reach_weight(my, TH, side * float(REACH - at)) for at in range(OFFSETS)]
+    weights = [reach_weight(my, TH, side * float(at - REACH)) for at in range(OFFSETS)]
 
     def band(part):
         acc = None
@@ -422,11 +422,11 @@
 
 
 def narrow_pieces(mine):
+    below1 = swap(mine, 1)
     above1 = swap(mine, 0)
-    below1 = swap(mine, 1)
     above2 = swap(below1, 0)
     below2 = swap(above1, 1)
-    return [below2, below1, mine, above1, above2]
+    return [above2, above1, mine, below1, below2]
 
 
 def local(amplitude, tilt, owner, row_offset, col_offset):

time: 90.6 us -> 92.2 us (1.018)
  waiting for transfers between devices: 23.5 us -> 24.7 us
    ppermute x8, waiting for transfers between devices: 7.47 us -> 8.65 us  [swap(): lax.ppermute(value, 'narrow', pairs + [(high, low) for low, high in pairs])]
  transfers between devices with their start and end apart: 9 -> 9, of which waited for: 3 -> 6; matrix products, arithmetic and copies ran while one was open for 0% -> 0% of each run, Pallas kernels for 3% -> 3%
where the time goes in v4:
time: 92.2 us; the launch traced here: 91.7 us
  starting transfers between devices  50.5 us (55%)
  waiting for transfers between devices  24.7 us (27%)
  Pallas kernels  15.6 us (17%)
    ppermute x8, starting transfers between devices, swap(): lax.ppermute(value, 'narrow', pairs + [(high, low) for low, high in pairs])  37.9 us
    all_to_all x1, waiting for transfers between devices, local(): lax.all_to_all(outgoing.reshape(wide_count, ROWS, 256), 'wide', split_axi...  16 us
    all_to_all x1, starting transfers between devices, local(): lax.all_to_all(outgoing.reshape(wide_count, ROWS, 256), 'wide', split_axi...  12.6 us
    ppermute x8, waiting for transfers between devices, swap(): lax.ppermute(value, 'narrow', pairs + [(high, low) for low, high in pairs])  8.65 us
    pallas_call x1, Pallas kernels, column_sums(): pl.pallas_call(column_kernel, out_shape=(jax.ShapeDtypeStruct((2, TW, HAL...  8.21 us
    pallas_call x1, Pallas kernels, pack(): pl.pallas_call(pack_kernel, out_shape=jax.ShapeDtypeStruct((wide_count *...  2.76 us
    pallas_call x2, Pallas kernels, image_of(): pl.pallas_call(functools.partial(image_kernel, half), out_shape=jax.Shape...  2.68 us
  transfers between devices with their start and end apart: 9, of which 6 were waited for; matrix products, arithmetic and copies ran while one was open for 0% of the time, Pallas kernels for 3%

profile of v4, /device:TPU:22, one launch (start us, length us, event | category | flops | bytes accessed | tf_op | source)
XLA Modules:
  0.0 91.7 jit_solution(17521983919615982755)
XLA Ops:
  0.0 2.8 %pack.1 = bf16[1024,256]{1,0:T(8,128)(2,1)} custom-call(f32[64,256]{1,0:T(8,128)} %amp_at.1, f32[3,64]{1,0:T(4,128)} %tilt_at.1, s32[1,64]{1,0:T(1,128)} %bitcast.7, s32[1,64]{1,0:T(1,128)} %bitcast.8, s32[1,64]{1,0:T(1,128)} %bitcast.9), custom_call_target="tpu_custom_call" | custom-call | tf_op jit(solution)/shard_map/pack/pallas_call | solution.py:204
  2.8 12.6 %all-to-all-start = ((bf16[64,16,256]{2,1,0:T(8,128)(2,1)}), bf16[64,16,256]{2,1,0:T(8,128)(2,1)S(1)}, u32[]{:S(2)}, u32[]{:S(2)}) async-start(bf16[64,16,256]{2,1,0:T(8,128)(2,1)} %bitcast.6), calls=%async_computation | async-start | bytes 1048576 | tf_op jit(solution)/shard_map/all_to_all | solution.py:436
  15.4 1.5 %tables.1 = (bf16[1024,512]{1,0:T(8,128)(2,1)S(1)}, bf16[512,512]{1,0:T(8,128)(2,1)S(1)}, bf16[512,512]{1,0:T(8,128)(2,1)S(1)}, bf16[512,256]{1,0:T(8,128)(2,1)S...) custom-call(), custom_call_target="tpu_custom_call" | custom-call | flops 8000000 | bytes 3145728 | tf_op jit(solution)/shard_map/tables/pallas_call | solution.py:109
  16.9 0.0 copy-start
  16.9 0.8 copy-done
  17.7 16.0 %all-to-all-done = bf16[64,16,256]{2,1,0:T(8,128)(2,1)S(1)} async-done(((bf16[64,16,256]{2,1,0:T(8,128)(2,1)}), bf16[64,16,256]{2,1,0:T(8,128)(2,1)S(1)}, u32[]{:S(2)}, u32[]{:S(2)}) %all-to-all-start) | async-done | bytes 524320 | tf_op jit(solution)/shard_map/all_to_all | solution.py:436
  33.7 0.0 copy-start.1
  33.7 8.2 %column_sums.1 = (bf16[2,256,256]{2,1,0:T(8,128)(2,1)S(1)}, bf16[512,512]{1,0:T(8,128)(2,1)S(1)}) custom-call(bf16[1024,256]{1,0:T(8,128)(2,1)S(1)} %bitcast.5, bf16[1024,512]{1,0:T(8,128)(2,1)S(1)} %get-tuple-element.14.lead_ref), custom_call_target="tpu_custom_call" | custom-call | flops 6000000000 | bytes 3145728 | tf_op jit(solution)/shard_map/column_sums/pallas_call | solution.py:322
  41.9 18.0 %collective-permute-start.4 = (bf16[2,256,256]{2,1,0:T(8,128)(2,1)S(1)}, bf16[2,256,256]{2,1,0:T(8,128)(2,1)S(1)}, u32[]{:S(2)}, u32[]{:S(2)}) collective-permute-start(bf16[2,256,256]{2,1,0:T(8,128)(2,1)S(1)} %get-tuple-element.20.refs_2_), channel_id=1, source_target_pairs={{1,2},{3,4},{5,6},{7,8},{9,10},{11,12},{13,14},{2,1},{4,3},{6,5},{... | collective-permute-start | bytes 786440 | tf_op jit(solution)/shard_map/ppermute | solution.py:421
  59.9 1.9 %collective-permute-start.6 = (bf16[2,256,256]{2,1,0:T(8,128)(2,1)S(1)}, bf16[2,256,256]{2,1,0:T(8,128)(2,1)S(1)}, u32[]{:S(2)}, u32[]{:S(2)}) collective-permute-start(bf16[2,256,256]{2,1,0:T(8,128)(2,1)S(1)} %get-tuple-element.20.refs_2_), channel_id=1, source_target_pairs={{0,1},{2,3},{4,5},{6,7},{8,9},{10,11},{12,13},{14,15},{1,0},{3,2},... | collective-permute-start | bytes 786440 | tf_op jit(solution)/shard_map/ppermute | solution.py:421
  61.8 0.0 copy-done.1
  61.9 0.4 second_half.1.refs_2_
  62.3 1.9 %collective-permute-start = (bf16[2,256,256]{2,1,0:T(8,128)(2,1)S(1)}, bf16[2,256,256]{2,1,0:T(8,128)(2,1)S(1)}, u32[]{:S(2)}, u32[]{:S(2)}) collective-permute-start(bf16[2,256,256]{2,1,0:T(8,128)(2,1)S(1)} %second_half.1.refs_2_), channel_id=1, source_target_pairs={{1,2},{3,4},{5,6},{7,8},{9,10},{11,12},{13,14},{2,1},{4,3},{6,5},{... | collective-permute-start | bytes 786440 | tf_op jit(solution)/shard_map/ppermute | solution.py:421
  64.2 3.9 %collective-permute-start.2 = (bf16[2,256,256]{2,1,0:T(8,128)(2,1)S(1)}, bf16[2,256,256]{2,1,0:T(8,128)(2,1)S(1)}, u32[]{:S(2)}, u32[]{:S(2)}) collective-permute-start(bf16[2,256,256]{2,1,0:T(8,128)(2,1)S(1)} %second_half.1.refs_2_), channel_id=1, source_target_pairs={{0,1},{2,3},{4,5},{6,7},{8,9},{10,11},{12,13},{14,15},{1,0},{3,2},... | collective-permute-start | bytes 786440 | tf_op jit(solution)/shard_map/ppermute | solution.py:421
  68.2 0.0 collective-permute-done.4.refs_3_
  68.2 1.9 %collective-permute-start.5 = (bf16[2,256,256]{2,1,0:T(8,128)(2,1)S(1)}, bf16[2,256,256]{2,1,0:T(8,128)(2,1)S(1)}, u32[]{:S(2)}, u32[]{:S(2)}) collective-permute-start(bf16[2,256,256]{2,1,0:T(8,128)(2,1)S(1)} %collective-permute-done.4.refs_3_), channel_id=1, source_target_pairs={{0,1},{2,3},{4,5},{6,7},{8,9},{10,11},{12,13},{14,15},{1,0},{3,2},... | collective-permute-start | bytes 786440 | tf_op jit(solution)/shard_map/ppermute | solution.py:421
  70.1 0.9 collective-permute-done.6.refs_1_
  71.0 5.1 %collective-permute-start.7 = (bf16[2,256,256]{2,1,0:T(8,128)(2,1)S(1)}, bf16[2,256,256]{2,1,0:T(8,128)(2,1)S(1)}, u32[]{:S(2)}, u32[]{:S(2)}) collective-permute-start(bf16[2,256,256]{2,1,0:T(8,128)(2,1)S(1)} %collective-permute-done.6.refs_1_), channel_id=1, source_target_pairs={{1,2},{3,4},{5,6},{7,8},{9,10},{11,12},{13,14},{2,1},{4,3},{6,5},{... | collective-permute-start | bytes 786440 | tf_op jit(solution)/shard_map/ppermute | solution.py:421
  76.1 0.0 collective-permute-done.refs_3_
  76.2 1.9 %collective-permute-start.1 = (bf16[2,256,256]{2,1,0:T(8,128)(2,1)S(1)}, bf16[2,256,256]{2,1,0:T(8,128)(2,1)S(1)}, u32[]{:S(2)}, u32[]{:S(2)}) collective-permute-start(bf16[2,256,256]{2,1,0:T(8,128)(2,1)S(1)} %collective-permute-done.refs_3_), channel_id=1, source_target_pairs={{0,1},{2,3},{4,5},{6,7},{8,9},{10,11},{12,13},{14,15},{1,0},{3,2},... | collective-permute-start | bytes 786440 | tf_op jit(solution)/shard_map/ppermute | solution.py:421
  78.1 0.0 collective-permute-done.2.refs_1_
  78.1 3.2 %collective-permute-start.3 = (bf16[2,256,256]{2,1,0:T(8,128)(2,1)S(1)}, bf16[2,256,256]{2,1,0:T(8,128)(2,1)S(1)}, u32[]{:S(2)}, u32[]{:S(2)}) collective-permute-start(bf16[2,256,256]{2,1,0:T(8,128)(2,1)S(1)} %collective-permute-done.2.refs_1_), channel_id=1, source_target_pairs={{1,2},{3,4},{5,6},{7,8},{9,10},{11,12},{13,14},{2,1},{4,3},{6,5},{... | collective-permute-start | bytes 786440 | tf_op jit(solution)/shard_map/ppermute | solution.py:421
  81.3 1.0 %collective-permute-done.5.refs_0_ = bf16[2,256,256]{2,1,0:T(8,128)(2,1)S(1)} collective-permute-done((bf16[2,256,256]{2,1,0:T(8,128)(2,1)S(1)}, bf16[2,256,256]{2,1,0:T(8,128)(2,1)S(1)}, u32[]{:S(2)}, u32[]{:S(2)}) %collective-permute-start.5) | collective-permute-done | bytes 262176 | tf_op jit(solution)/shard_map/ppermute | solution.py:421
  82.2 0.5 collective-permute-done.7.refs_4_
  82.7 0.9 image.2.refs_8_
  83.6 3.9 %collective-permute-done.1.refs_0_ = bf16[2,256,256]{2,1,0:T(8,128)(2,1)S(1)} collective-permute-done((bf16[2,256,256]{2,1,0:T(8,128)(2,1)S(1)}, bf16[2,256,256]{2,1,0:T(8,128)(2,1)S(1)}, u32[]{:S(2)}, u32[]{:S(2)}) %collective-permute-start.1) | collective-permute-done | bytes 262176 | tf_op jit(solution)/shard_map/ppermute | solution.py:421
  87.6 2.3 %collective-permute-done.3.refs_4_ = bf16[2,256,256]{2,1,0:T(8,128)(2,1)S(1)} collective-permute-done((bf16[2,256,256]{2,1,0:T(8,128)(2,1)S(1)}, bf16[2,256,256]{2,1,0:T(8,128)(2,1)S(1)}, u32[]{:S(2)}, u32[]{:S(2)}) %collective-permute-start.3) | collective-permute-done | bytes 262176 | tf_op jit(solution)/shard_map/ppermute | solution.py:421
  89.9 1.8 %image.3 = f32[2,512,256]{2,1,0:T(8,128)} custom-call(bf16[2,256,256]{2,1,0:T(8,128)(2,1)S(1)} %collective-permute-done.1.refs_0_, bf16[2,256,256]{2,1,0:T(8,128)(2,1)S(1)} %collective-permute-done.2.refs_1_, bf16[2,256,256]{2,1,0:T(8,128)(2,1)S(1)} %second_half.1.refs_2_, bf16[2,256,256]{2,1,0:T(8,128)(2,1)S(1)} %collective-permute-done.refs_3_, ...), custom_call_target="tpu_custom_call" | custom-call | flops 900000000 | bytes 4194304 | tf_op jit(solution)/shard_map/image/pallas_call | solution.py:406
Async XLA Ops:
  2.8 31.0 %all-to-all-start = ((bf16[64,16,256]{2,1,0:T(8,128)(2,1)}), bf16[64,16,256]{2,1,0:T(8,128)(2,1)S(1)}, u32[]{:S(2)}, u32[]{:S(2)}) async-start(bf16[64,16,256]{2,1,0:T(8,128)(2,1)} %bitcast.6), calls=%async_computation | async-start | bytes 1048576 | tf_op jit(solution)/shard_map/all_to_all | solution.py:436
  16.9 0.8 copy-start
  33.7 28.1 %copy-start.1 = (bf16[512,512]{1,0:T(8,128)(2,1)S(1)}, bf16[512,512]{1,0:T(8,128)(2,1)}, u32[]{:S(2)}) copy-start(bf16[512,512]{1,0:T(8,128)(2,1)} %copy-done) | copy-start | bytes 1572868
  41.9 26.2 %collective-permute-start.4 = (bf16[2,256,256]{2,1,0:T(8,128)(2,1)S(1)}, bf16[2,256,256]{2,1,0:T(8,128)(2,1)S(1)}, u32[]{:S(2)}, u32[]{:S(2)}) collective-permute-start(bf16[2,256,256]{2,1,0:T(8,128)(2,1)S(1)} %get-tuple-element.20.refs_2_), channel_id=1, source_target_pairs={{1,2},{3,4},{5,6},{7,8},{9,10},{11,12},{13,14},{2,1},{4,3},{6,5},{... | collective-permute-start | bytes 786440 | tf_op jit(solution)/shard_map/ppermute | solution.py:421
  59.9 11.1 %collective-permute-start.6 = (bf16[2,256,256]{2,1,0:T(8,128)(2,1)S(1)}, bf16[2,256,256]{2,1,0:T(8,128)(2,1)S(1)}, u32[]{:S(2)}, u32[]{:S(2)}) collective-permute-start(bf16[2,256,256]{2,1,0:T(8,128)(2,1)S(1)} %get-tuple-element.20.refs_2_), channel_id=1, source_target_pairs={{0,1},{2,3},{4,5},{6,7},{8,9},{10,11},{12,13},{14,15},{1,0},{3,2},... | collective-permute-start | bytes 786440 | tf_op jit(solution)/shard_map/ppermute | solution.py:421
  62.3 13.8 %collective-permute-start = (bf16[2,256,256]{2,1,0:T(8,128)(2,1)S(1)}, bf16[2,256,256]{2,1,0:T(8,128)(2,1)S(1)}, u32[]{:S(2)}, u32[]{:S(2)}) collective-permute-start(bf16[2,256,256]{2,1,0:T(8,128)(2,1)S(1)} %second_half.1.refs_2_), channel_id=1, source_target_pairs={{1,2},{3,4},{5,6},{7,8},{9,10},{11,12},{13,14},{2,1},{4,3},{6,5},{... | collective-permute-start | bytes 786440 | tf_op jit(solution)/shard_map/ppermute | solution.py:421
  64.2 13.9 %collective-permute-start.2 = (bf16[2,256,256]{2,1,0:T(8,128)(2,1)S(1)}, bf16[2,256,256]{2,1,0:T(8,128)(2,1)S(1)}, u32[]{:S(2)}, u32[]{:S(2)}) collective-permute-start(bf16[2,256,256]{2,1,0:T(8,128)(2,1)S(1)} %second_half.1.refs_2_), channel_id=1, source_target_pairs={{0,1},{2,3},{4,5},{6,7},{8,9},{10,11},{12,13},{14,15},{1,0},{3,2},... | collective-permute-start | bytes 786440 | tf_op jit(solution)/shard_map/ppermute | solution.py:421
  68.2 14.1 %collective-permute-start.5 = (bf16[2,256,256]{2,1,0:T(8,128)(2,1)S(1)}, bf16[2,256,256]{2,1,0:T(8,128)(2,1)S(1)}, u32[]{:S(2)}, u32[]{:S(2)}) collective-permute-start(bf16[2,256,256]{2,1,0:T(8,128)(2,1)S(1)} %collective-permute-done.4.refs_3_), channel_id=1, source_target_pairs={{0,1},{2,3},{4,5},{6,7},{8,9},{10,11},{12,13},{14,15},{1,0},{3,2},... | collective-permute-start | bytes 786440 | tf_op jit(solution)/shard_map/ppermute | solution.py:421
  71.0 11.8 %collective-permute-start.7 = (bf16[2,256,256]{2,1,0:T(8,128)(2,1)S(1)}, bf16[2,256,256]{2,1,0:T(8,128)(2,1)S(1)}, u32[]{:S(2)}, u32[]{:S(2)}) collective-permute-start(bf16[2,256,256]{2,1,0:T(8,128)(2,1)S(1)} %collective-permute-done.6.refs_1_), channel_id=1, source_target_pairs={{1,2},{3,4},{5,6},{7,8},{9,10},{11,12},{13,14},{2,1},{4,3},{6,5},{... | collective-permute-start | bytes 786440 | tf_op jit(solution)/shard_map/ppermute | solution.py:421
  76.2 11.4 %collective-permute-start.1 = (bf16[2,256,256]{2,1,0:T(8,128)(2,1)S(1)}, bf16[2,256,256]{2,1,0:T(8,128)(2,1)S(1)}, u32[]{:S(2)}, u32[]{:S(2)}) collective-permute-start(bf16[2,256,256]{2,1,0:T(8,128)(2,1)S(1)} %collective-permute-done.refs_3_), channel_id=1, source_target_pairs={{0,1},{2,3},{4,5},{6,7},{8,9},{10,11},{12,13},{14,15},{1,0},{3,2},... | collective-permute-start | bytes 786440 | tf_op jit(solution)/shard_map/ppermute | solution.py:421
  78.1 11.8 %collective-permute-start.3 = (bf16[2,256,256]{2,1,0:T(8,128)(2,1)S(1)}, bf16[2,256,256]{2,1,0:T(8,128)(2,1)S(1)}, u32[]{:S(2)}, u32[]{:S(2)}) collective-permute-start(bf16[2,256,256]{2,1,0:T(8,128)(2,1)S(1)} %collective-permute-done.2.refs_1_), channel_id=1, source_target_pairs={{1,2},{3,4},{5,6},{7,8},{9,10},{11,12},{13,14},{2,1},{4,3},{6,5},{... | collective-permute-start | bytes 786440 | tf_op jit(solution)/shard_map/ppermute | solution.py:421

commit v5 on v2

--- a/solution.py
+++ b/solution.py
@@ -340,25 +340,30 @@
     )(incoming, lead)
 
 
-def second_kernel(value_ref, grow_ref, out_ref):
+def second_kernel(value_ref, grow_ref, first_ref, out_ref, both_ref):
     row_transform(value_ref[...], grow_ref, out_ref)
-
-
-def second_half(value, grow):
+    both_ref[0] = first_ref[...]
+    both_ref[1] = out_ref[...]
+
+
+def second_half(value, grow, first):
     return pl.pallas_call(
         second_kernel,
-        out_shape=jax.ShapeDtypeStruct((2, TW, HALF), BF16),
-        in_specs=[pl.BlockSpec(memory_space=pltpu.VMEM)] * 2,
-        out_specs=pl.BlockSpec(memory_space=pltpu.VMEM),
+        out_shape=(
+            jax.ShapeDtypeStruct((2, TW, HALF), BF16),
+            jax.ShapeDtypeStruct((2, 2, TW, HALF), BF16),
+        ),
+        in_specs=[pl.BlockSpec(memory_space=pltpu.VMEM)] * 3,
+        out_specs=tuple([pl.BlockSpec(memory_space=pltpu.VMEM)] * 2),
         compiler_params=pltpu.CompilerParams(vmem_limit_bytes=8 << 20),
         cost_estimate=pl.CostEstimate(flops=600_000_000, bytes_accessed=2 << 20, transcendentals=0),
         name="second_half",
-    )(value, grow)
+    )(value, grow, first)
 
 
 def image_kernel(half, *refs):
     side = (1 - 2 * (lax.axis_index("narrow") & 1)).astype(F32)
-    pieces = refs[:OFFSETS]
+    pieces = [refs[0], refs[1], refs[2], refs[3].at[half], refs[4]]
     hblk_ref, kr_ref, ki_ref = refs[OFFSETS : OFFSETS + 3]
     my = iota((1, HALF), 1) + HALF * half
     weights = [reach_weight(my, TH, side * float(REACH - at)) for at in range(OFFSETS)]
@@ -421,12 +426,15 @@
     return lax.ppermute(value, "narrow", pairs + [(high, low) for low, high in pairs])
 
 
-def narrow_pieces(mine):
-    above1 = swap(mine, 0)
-    below1 = swap(mine, 1)
-    above2 = swap(below1, 0)
-    below2 = swap(above1, 1)
-    return [below2, below1, mine, above1, above2]
+def narrow_pieces(both, halves):
+    above1 = swap(both, 0)
+    pieces = []
+    for half, mine in enumerate(halves):
+        below1 = swap(mine, 1)
+        above2 = swap(below1, 0)
+        below2 = swap(above1[half], 1)
+        pieces.append([below2, below1, mine, above1, above2])
+    return pieces
 
 
 def local(amplitude, tilt, owner, row_offset, col_offset):
@@ -437,9 +445,10 @@
         outgoing.reshape(wide_count, ROWS, 256), "wide", split_axis=0, concat_axis=0, tiled=True
     ).reshape(wide_count * ROWS, 256)
     first, value = column_sums(incoming, lead)
-    second = second_half(value, grow_b)
-    partial = image_of(0, narrow_pieces(first), (hblk, kr_a, ki_a), ())
-    return image_of(1, narrow_pieces(second), (hblk, kr_b, ki_b), (partial,))
+    second, both = second_half(value, grow_b, first)
+    pieces = narrow_pieces(both, (first, second))
+    partial = image_of(0, pieces[0], (hblk, kr_a, ki_a), ())
+    return image_of(1, pieces[1], (hblk, kr_b, ki_b), (partial,))
 
 
 def solution(mesh):

time: 90.6 us -> 93.6 us (1.033)
  waiting for transfers between devices: 23.5 us -> 28.2 us
  starting transfers between devices: 50.2 us -> 48.5 us
    ppermute x8 -> x7, waiting for transfers between devices: 7.47 us -> 12.2 us  [swap(): lax.ppermute(value, 'narrow', pairs + [(high, low) for low, high in pairs])]
    ppermute x8 -> x7, starting transfers between devices: 37.5 us -> 35.9 us  [swap(): lax.ppermute(value, 'narrow', pairs + [(high, low) for low, high in pairs])]
  transfers between devices with their start and end apart: 9 -> 8, of which waited for: 3 -> 5; matrix products, arithmetic and copies ran while one was open for 0% -> 0% of each run, Pallas kernels for 3% -> 3%
where the time goes in v5:
time: 93.6 us; the launch traced here: 93.2 us
  starting transfers between devices  48.5 us (52%)
  waiting for transfers between devices  28.2 us (30%)
  Pallas kernels  15.6 us (17%)
    ppermute x7, starting transfers between devices, swap(): lax.ppermute(value, 'narrow', pairs + [(high, low) for low, high in pairs])  35.9 us
    all_to_all x1, waiting for transfers between devices, local(): lax.all_to_all(outgoing.reshape(wide_count, ROWS, 256), 'wide', split_axi...  16 us
    all_to_all x1, starting transfers between devices, local(): lax.all_to_all(outgoing.reshape(wide_count, ROWS, 256), 'wide', split_axi...  12.6 us
    ppermute x7, waiting for transfers between devices, swap(): lax.ppermute(value, 'narrow', pairs + [(high, low) for low, high in pairs])  12.2 us
    pallas_call x1, Pallas kernels, column_sums(): pl.pallas_call(column_kernel, out_shape=(jax.ShapeDtypeStruct((2, TW, HAL...  8.21 us
    pallas_call x1, Pallas kernels, pack(): pl.pallas_call(pack_kernel, out_shape=jax.ShapeDtypeStruct((wide_count *...  2.76 us
    pallas_call x2, Pallas kernels, image_of(): pl.pallas_call(functools.partial(image_kernel, half), out_shape=jax.Shape...  2.68 us
  transfers between devices with their start and end apart: 8, of which 5 were waited for; matrix products, arithmetic and copies ran while one was open for 0% of the time, Pallas kernels for 3%

profile of v5, /device:TPU:22, one launch (start us, length us, event | category | flops | bytes accessed | tf_op | source)
XLA Modules:
  0.0 93.2 jit_solution(2647894319421532517)
XLA Ops:
  0.0 2.8 %pack.1 = bf16[1024,256]{1,0:T(8,128)(2,1)} custom-call(f32[64,256]{1,0:T(8,128)} %amp_at.1, f32[3,64]{1,0:T(4,128)} %tilt_at.1, s32[1,64]{1,0:T(1,128)} %bitcast.11, s32[1,64]{1,0:T(1,128)} %bitcast.12, s32[1,64]{1,0:T(1,128)} %bitcast.13), custom_call_target="tpu_custom_call" | custom-call | tf_op jit(solution)/shard_map/pack/pallas_call | solution.py:204
  2.8 12.6 %all-to-all-start = ((bf16[64,16,256]{2,1,0:T(8,128)(2,1)}), bf16[64,16,256]{2,1,0:T(8,128)(2,1)S(1)}, u32[]{:S(2)}, u32[]{:S(2)}) async-start(bf16[64,16,256]{2,1,0:T(8,128)(2,1)} %bitcast.10), calls=%async_computation | async-start | bytes 1048576 | tf_op jit(solution)/shard_map/all_to_all | solution.py:444
  15.4 1.5 %tables.1 = (bf16[1024,512]{1,0:T(8,128)(2,1)S(1)}, bf16[512,512]{1,0:T(8,128)(2,1)S(1)}, bf16[512,512]{1,0:T(8,128)(2,1)S(1)}, bf16[512,256]{1,0:T(8,128)(2,1)S...) custom-call(), custom_call_target="tpu_custom_call" | custom-call | flops 8000000 | bytes 3145728 | tf_op jit(solution)/shard_map/tables/pallas_call | solution.py:109
  16.9 0.0 copy-start
  16.9 0.8 copy-done
  17.7 16.0 %all-to-all-done = bf16[64,16,256]{2,1,0:T(8,128)(2,1)S(1)} async-done(((bf16[64,16,256]{2,1,0:T(8,128)(2,1)}), bf16[64,16,256]{2,1,0:T(8,128)(2,1)S(1)}, u32[]{:S(2)}, u32[]{:S(2)}) %all-to-all-start) | async-done | bytes 524320 | tf_op jit(solution)/shard_map/all_to_all | solution.py:444
  33.7 0.0 copy-start.1
  33.7 8.2 %column_sums.1 = (bf16[2,256,256]{2,1,0:T(8,128)(2,1)S(1)}, bf16[512,512]{1,0:T(8,128)(2,1)S(1)}) custom-call(bf16[1024,256]{1,0:T(8,128)(2,1)S(1)} %bitcast.9, bf16[1024,512]{1,0:T(8,128)(2,1)S(1)} %get-tuple-element.16.lead_ref), custom_call_target="tpu_custom_call" | custom-call | flops 6000000000 | bytes 3145728 | tf_op jit(solution)/shard_map/column_sums/pallas_call | solution.py:322
  41.9 0.0 copy-done.1
  42.0 0.4 second_half.1
  42.4 5.2 %collective-permute-start = (bf16[2,2,256,256]{3,2,1,0:T(8,128)(2,1)S(1)}, bf16[2,2,256,256]{3,2,1,0:T(8,128)(2,1)S(1)}, u32[]{:S(2)}, u32[]{:S(2)}) collective-permute-start(bf16[2,2,256,256]{3,2,1,0:T(8,128)(2,1)S(1)} %get-tuple-element.20), channel_id=1, source_target_pairs={{0,1},{2,3},{4,5},{6,7},{8,9},{10,11},{12,13},{14,15},{1,0},{3,2},... | collective-permute-start | bytes 1572872 | tf_op jit(solution)/shard_map/ppermute | solution.py:426
  47.6 14.7 %collective-permute-start.5 = (bf16[2,256,256]{2,1,0:T(8,128)(2,1)S(1)}, bf16[2,256,256]{2,1,0:T(8,128)(2,1)S(1)}, u32[]{:S(2)}, u32[]{:S(2)}) collective-permute-start(bf16[2,256,256]{2,1,0:T(8,128)(2,1)S(1)} %get-tuple-element.19.first_ref.refs_2_), channel_id=1, source_target_pairs={{1,2},{3,4},{5,6},{7,8},{9,10},{11,12},{13,14},{2,1},{4,3},{6,5},{... | collective-permute-start | bytes 786440 | tf_op jit(solution)/shard_map/ppermute | solution.py:426
  62.3 1.9 %collective-permute-start.2 = (bf16[2,256,256]{2,1,0:T(8,128)(2,1)S(1)}, bf16[2,256,256]{2,1,0:T(8,128)(2,1)S(1)}, u32[]{:S(2)}, u32[]{:S(2)}) collective-permute-start(bf16[2,256,256]{2,1,0:T(8,128)(2,1)S(1)} %get-tuple-element.21.refs_2_), channel_id=1, source_target_pairs={{1,2},{3,4},{5,6},{7,8},{9,10},{11,12},{13,14},{2,1},{4,3},{6,5},{... | collective-permute-start | bytes 786440 | tf_op jit(solution)/shard_map/ppermute | solution.py:426
  64.2 4.9 %collective-permute-done.5.refs_1_ = bf16[2,256,256]{2,1,0:T(8,128)(2,1)S(1)} collective-permute-done((bf16[2,256,256]{2,1,0:T(8,128)(2,1)S(1)}, bf16[2,256,256]{2,1,0:T(8,128)(2,1)S(1)}, u32[]{:S(2)}, u32[]{:S(2)}) %collective-permute-start.5) | collective-permute-done | bytes 262176 | tf_op jit(solution)/shard_map/ppermute | solution.py:426
  69.2 1.9 %collective-permute-start.6 = (bf16[2,256,256]{2,1,0:T(8,128)(2,1)S(1)}, bf16[2,256,256]{2,1,0:T(8,128)(2,1)S(1)}, u32[]{:S(2)}, u32[]{:S(2)}) collective-permute-start(bf16[2,256,256]{2,1,0:T(8,128)(2,1)S(1)} %collective-permute-done.5.refs_1_), channel_id=1, source_target_pairs={{0,1},{2,3},{4,5},{6,7},{8,9},{10,11},{12,13},{14,15},{1,0},{3,2},... | collective-permute-start | bytes 786440 | tf_op jit(solution)/shard_map/ppermute | solution.py:426
  71.1 0.0 collective-permute-done.refs_3_
  71.1 6.3 %collective-permute-start.4 = (bf16[2,256,256]{2,1,0:T(8,128)(2,1)S(1)}, bf16[2,256,256]{2,1,0:T(8,128)(2,1)S(1)}, u32[]{:S(2)}, u32[]{:S(2)}) collective-permute-start(bf16[2,256,256]{2,1,0:T(8,128)(2,1)S(1)} %get-tuple-element.27), channel_id=1, source_target_pairs={{1,2},{3,4},{5,6},{7,8},{9,10},{11,12},{13,14},{2,1},{4,3},{6,5},{... | collective-permute-start | bytes 786440 | tf_op jit(solution)/shard_map/ppermute | solution.py:426
  77.5 0.0 collective-permute-done.2.refs_1_
  77.5 1.9 %collective-permute-start.3 = (bf16[2,256,256]{2,1,0:T(8,128)(2,1)S(1)}, bf16[2,256,256]{2,1,0:T(8,128)(2,1)S(1)}, u32[]{:S(2)}, u32[]{:S(2)}) collective-permute-start(bf16[2,256,256]{2,1,0:T(8,128)(2,1)S(1)} %collective-permute-done.2.refs_1_), channel_id=1, source_target_pairs={{0,1},{2,3},{4,5},{6,7},{8,9},{10,11},{12,13},{14,15},{1,0},{3,2},... | collective-permute-start | bytes 786440 | tf_op jit(solution)/shard_map/ppermute | solution.py:426
  79.4 3.9 %collective-permute-start.1 = (bf16[2,256,256]{2,1,0:T(8,128)(2,1)S(1)}, bf16[2,256,256]{2,1,0:T(8,128)(2,1)S(1)}, u32[]{:S(2)}, u32[]{:S(2)}) collective-permute-start(bf16[2,256,256]{2,1,0:T(8,128)(2,1)S(1)} %get-tuple-element.28), channel_id=1, source_target_pairs={{1,2},{3,4},{5,6},{7,8},{9,10},{11,12},{13,14},{2,1},{4,3},{6,5},{... | collective-permute-start | bytes 786440 | tf_op jit(solution)/shard_map/ppermute | solution.py:426
  83.3 0.0 collective-permute-done.6.refs_4_
  83.3 0.7 collective-permute-done.4.refs_0_
  84.0 0.9 image.2.refs_8_
  84.9 2.5 %collective-permute-done.3.refs_4_ = bf16[2,256,256]{2,1,0:T(8,128)(2,1)S(1)} collective-permute-done((bf16[2,256,256]{2,1,0:T(8,128)(2,1)S(1)}, bf16[2,256,256]{2,1,0:T(8,128)(2,1)S(1)}, u32[]{:S(2)}, u32[]{:S(2)}) %collective-permute-start.3) | collective-permute-done | bytes 262176 | tf_op jit(solution)/shard_map/ppermute | solution.py:426
  87.4 4.0 %collective-permute-done.1.refs_0_ = bf16[2,256,256]{2,1,0:T(8,128)(2,1)S(1)} collective-permute-done((bf16[2,256,256]{2,1,0:T(8,128)(2,1)S(1)}, bf16[2,256,256]{2,1,0:T(8,128)(2,1)S(1)}, u32[]{:S(2)}, u32[]{:S(2)}) %collective-permute-start.1) | collective-permute-done | bytes 262176 | tf_op jit(solution)/shard_map/ppermute | solution.py:426
  91.4 1.8 %image.3 = f32[2,512,256]{2,1,0:T(8,128)} custom-call(bf16[2,256,256]{2,1,0:T(8,128)(2,1)S(1)} %collective-permute-done.1.refs_0_, bf16[2,256,256]{2,1,0:T(8,128)(2,1)S(1)} %collective-permute-done.2.refs_1_, bf16[2,256,256]{2,1,0:T(8,128)(2,1)S(1)} %get-tuple-element.21.refs_2_, bf16[2,2,256,256]{3,2,1,0:T(8,128)(2,1)S(1)} %collective-permute-done.refs_3_, ...), custom_call_target="tpu_custom_call" | custom-call | flops 900000000 | bytes 4194304 | tf_op jit(solution)/shard_map/image/pallas_call | solution.py:411
  (1 shorter events, 0.0 us)
Async XLA Ops:
  2.8 31.0 %all-to-all-start = ((bf16[64,16,256]{2,1,0:T(8,128)(2,1)}), bf16[64,16,256]{2,1,0:T(8,128)(2,1)S(1)}, u32[]{:S(2)}, u32[]{:S(2)}) async-start(bf16[64,16,256]{2,1,0:T(8,128)(2,1)} %bitcast.10), calls=%async_computation | async-start | bytes 1048576 | tf_op jit(solution)/shard_map/all_to_all | solution.py:444
  16.9 0.8 copy-start
  33.7 8.2 %copy-start.1 = (bf16[512,512]{1,0:T(8,128)(2,1)S(1)}, bf16[512,512]{1,0:T(8,128)(2,1)}, u32[]{:S(2)}) copy-start(bf16[512,512]{1,0:T(8,128)(2,1)} %copy-done) | copy-start | bytes 1572868
  42.4 28.7 %collective-permute-start = (bf16[2,2,256,256]{3,2,1,0:T(8,128)(2,1)S(1)}, bf16[2,2,256,256]{3,2,1,0:T(8,128)(2,1)S(1)}, u32[]{:S(2)}, u32[]{:S(2)}) collective-permute-start(bf16[2,2,256,256]{3,2,1,0:T(8,128)(2,1)S(1)} %get-tuple-element.20), channel_id=1, source_target_pairs={{0,1},{2,3},{4,5},{6,7},{8,9},{10,11},{12,13},{14,15},{1,0},{3,2},... | collective-permute-start | bytes 1572872 | tf_op jit(solution)/shard_map/ppermute | solution.py:426
  47.6 21.6 %collective-permute-start.5 = (bf16[2,256,256]{2,1,0:T(8,128)(2,1)S(1)}, bf16[2,256,256]{2,1,0:T(8,128)(2,1)S(1)}, u32[]{:S(2)}, u32[]{:S(2)}) collective-permute-start(bf16[2,256,256]{2,1,0:T(8,128)(2,1)S(1)} %get-tuple-element.19.first_ref.refs_2_), channel_id=1, source_target_pairs={{1,2},{3,4},{5,6},{7,8},{9,10},{11,12},{13,14},{2,1},{4,3},{6,5},{... | collective-permute-start | bytes 786440 | tf_op jit(solution)/shard_map/ppermute | solution.py:426
  62.3 15.2 %collective-permute-start.2 = (bf16[2,256,256]{2,1,0:T(8,128)(2,1)S(1)}, bf16[2,256,256]{2,1,0:T(8,128)(2,1)S(1)}, u32[]{:S(2)}, u32[]{:S(2)}) collective-permute-start(bf16[2,256,256]{2,1,0:T(8,128)(2,1)S(1)} %get-tuple-element.21.refs_2_), channel_id=1, source_target_pairs={{1,2},{3,4},{5,6},{7,8},{9,10},{11,12},{13,14},{2,1},{4,3},{6,5},{... | collective-permute-start | bytes 786440 | tf_op jit(solution)/shard_map/ppermute | solution.py:426
  69.2 14.2 %collective-permute-start.6 = (bf16[2,256,256]{2,1,0:T(8,128)(2,1)S(1)}, bf16[2,256,256]{2,1,0:T(8,128)(2,1)S(1)}, u32[]{:S(2)}, u32[]{:S(2)}) collective-permute-start(bf16[2,256,256]{2,1,0:T(8,128)(2,1)S(1)} %collective-permute-done.5.refs_1_), channel_id=1, source_target_pairs={{0,1},{2,3},{4,5},{6,7},{8,9},{10,11},{12,13},{14,15},{1,0},{3,2},... | collective-permute-start | bytes 786440 | tf_op jit(solution)/shard_map/ppermute | solution.py:426
  71.1 12.9 %collective-permute-start.4 = (bf16[2,256,256]{2,1,0:T(8,128)(2,1)S(1)}, bf16[2,256,256]{2,1,0:T(8,128)(2,1)S(1)}, u32[]{:S(2)}, u32[]{:S(2)}) collective-permute-start(bf16[2,256,256]{2,1,0:T(8,128)(2,1)S(1)} %get-tuple-element.27), channel_id=1, source_target_pairs={{1,2},{3,4},{5,6},{7,8},{9,10},{11,12},{13,14},{2,1},{4,3},{6,5},{... | collective-permute-start | bytes 786440 | tf_op jit(solution)/shard_map/ppermute | solution.py:426
  77.5 9.9 %collective-permute-start.3 = (bf16[2,256,256]{2,1,0:T(8,128)(2,1)S(1)}, bf16[2,256,256]{2,1,0:T(8,128)(2,1)S(1)}, u32[]{:S(2)}, u32[]{:S(2)}) collective-permute-start(bf16[2,256,256]{2,1,0:T(8,128)(2,1)S(1)} %collective-permute-done.2.refs_1_), channel_id=1, source_target_pairs={{0,1},{2,3},{4,5},{6,7},{8,9},{10,11},{12,13},{14,15},{1,0},{3,2},... | collective-permute-start | bytes 786440 | tf_op jit(solution)/shard_map/ppermute | solution.py:426
  79.4 12.0 %collective-permute-start.1 = (bf16[2,256,256]{2,1,0:T(8,128)(2,1)S(1)}, bf16[2,256,256]{2,1,0:T(8,128)(2,1)S(1)}, u32[]{:S(2)}, u32[]{:S(2)}) collective-permute-start(bf16[2,256,256]{2,1,0:T(8,128)(2,1)S(1)} %get-tuple-element.28), channel_id=1, source_target_pairs={{1,2},{3,4},{5,6},{7,8},{9,10},{11,12},{13,14},{2,1},{4,3},{6,5},{... | collective-permute-start | bytes 786440 | tf_op jit(solution)/shard_map/ppermute | solution.py:426
